TPU v7x, 32 devices: a whole 2x2x4 slice. The times are simulated.
32 devices in a mesh: grp: 2 (over core), seg: 16 (over z, y, x).
Axes of the slice: x: 2, y: 2, z: 4, core: 2. Of those that a mesh axis runs over, the one named last changes fastest.
Arguments:
- nodes: float32 [32, 256], P(('grp', 'seg')), may hold values from -6 to 6
- jac_inverse: float32 [128, 256, 256], P(('grp', 'seg')), may hold values from -3 to 3, as said below
- loss_rates: float32 [256], replicated, may hold values from 0.25 to 4
- rate_table: float32 [128, 256], P('grp'), may hold values from -6 to 6
- rate_index: int32 [128, 256], P(('grp', 'seg')), may hold values from 0 to 127
Outputs:
- new_nodes: float32 [32, 256], P(('grp', 'seg'))
- defects: float32 [32, 256], P(('grp', 'seg'))
Inputs may be any that keep to these rules, and one draw needn't show every extreme that they name: `jac_inverse`: one 256 x 256 matrix a step.
All inputs are finite; a program needn't handle non-finite values.
Results may differ from a plain program's by a relative error of at most 0.0003.
Values sent between devices are 32-bit elements; how exact they have to be, the bound alone decides.
No kernel may reach another device: no remote copies, remote signals or barrier semaphores. Data moves between devices by JAX's collectives and lax.ppermute only.
A program may use at most 192 MiB of HBM per device.

v0:
```python
import functools
import jax
import jax.numpy as jnp
from jax import lax
from jax.experimental import pallas as pl
from jax.experimental.pallas import tpu as pltpu
from jax.sharding import PartitionSpec as P


AXES = ("grp", "seg")
PAD = 8
QUAD = 4
VMEM = pl.BlockSpec(memory_space=pltpu.VMEM)
HBM = pl.BlockSpec(memory_space=pltpu.HBM)
F32 = jnp.float32


def halves(a):
    high = a.astype(jnp.bfloat16)
    return high, (a - high.astype(jnp.float32)).astype(jnp.bfloat16)


def dot(a, b, dims=((1,), (0,))):
    def one(x, y):
        return lax.dot_general(
            x, y, (dims, ((), ())), preferred_element_type=jnp.float32
        )

    (ah, al), (bh, bl) = halves(a), halves(b)
    return one(ah, bh) + (one(ah, bl) + one(al, bh))


def times(row, mat):
    n = mat.shape[0]
    on = lax.broadcasted_iota(jnp.int32, (n, n), 0) == lax.broadcasted_iota(
        jnp.int32, (n, n), 1
    )
    column = jnp.sum(jnp.where(on, row, 0.0), axis=1, keepdims=True)
    return jnp.sum(mat * column, axis=0, keepdims=True)


def call(body, shapes, *args, scratch=(), raw=False):
    out = tuple(jax.ShapeDtypeStruct(*s) for s in shapes)
    return pl.pallas_call(
        body,
        out_shape=out,
        in_specs=[HBM if raw else VMEM] * len(args),
        out_specs=tuple(VMEM for _ in out),
        scratch_shapes=list(scratch),
        compiler_params=pltpu.CompilerParams(vmem_limit_bytes=8 << 20),
    )(*args)


def where_am_i():
    return lax.axis_index("grp") * lax.axis_size("seg") + lax.axis_index("seg")


def put_composed(ref, earlier, later):
    width = later.shape[1]
    both = dot(earlier, later[:width])
    ref[:width] = both[:width]
    ref[width:] = both[width:] + later[width:]


def lookup(table, index, base):
    rows, width = table.shape
    level = lax.broadcasted_iota(jnp.int32, (rows, width), 0) + base
    kept = table[...]
    found = [
        jnp.sum(jnp.where(index[k : k + 1, :] == level, kept, 0.0), axis=0, keepdims=True)
        for k in range(index.shape[0])
    ]
    return jnp.concatenate(found, axis=0)


def early_body(
    inv_len, nodes_in, loss_in, jac_in, own_in, index_in,
    nodes, loss, jac, index, near, sens, state, own, sems,
):
    steps, width, _ = jac.shape
    copies = [
        pltpu.make_async_copy(src, dst, sems.at[k])
        for k, (src, dst) in enumerate(
            [(nodes_in, nodes), (loss_in, loss), (jac_in.at[0], jac.at[0])]
            + [(own_in, own), (index_in, index)]
            + [(jac_in.at[pl.ds(1, steps - 1)], jac.at[pl.ds(1, steps - 1)])]
        )
    ]
    for copy in copies:
        copy.start()
    for copy in copies[:3]:
        copy.wait()
    start = jnp.broadcast_to(nodes[...], (PAD, width))
    rates = loss[...]
    slope = jnp.tanh(start)
    weight = inv_len * (rates * (1.0 - slope * slope))
    row = lax.broadcasted_iota(jnp.int32, (width, width), 0)
    col = lax.broadcasted_iota(jnp.int32, (width, width), 1)
    first = jnp.where(row == col, weight[:1], 0.0)
    both = dot(
        jnp.concatenate([first, -inv_len * rates * slope], axis=0), jac[0], ((1,), (1,))
    )
    sens[...] = jnp.where(row == col, 1.0, 0.0) - both[:width]
    state[...] = start + both[width:]
    for copy in copies[3:5]:
        copy.wait()
    near[...] = lookup(own, index, lax.axis_index("grp") * own.shape[0])
    copies[5].wait()


def local_body(
    inv_len, src_scale, other, nodes, loss, jac, index, near, sens_in, state_in,
    out, final, kept,
):
    steps, width, _ = jac.shape
    rows = other.shape[0]
    source = near[...] + lookup(other, index, (1 - lax.axis_index("grp")) * rows)
    rates = loss[...]
    sens = sens_in[...]
    spread = jnp.sum(jac[0] * (src_scale * source[:1]), axis=1, keepdims=True)
    on = lax.broadcasted_iota(jnp.int32, (width, width), 0) == lax.broadcasted_iota(
        jnp.int32, (width, width), 1
    )
    state = state_in[...] + jnp.sum(jnp.where(on, spread, 0.0), axis=0, keepdims=True)
    for step in range(1, steps):
        slope = jnp.tanh(state)
        weight = inv_len * (rates * (1.0 - slope * slope))
        drive = src_scale * source[step : step + 1] - inv_len * rates * slope
        both = dot(
            jnp.concatenate([sens * weight[:1], drive], axis=0), jac[step], ((1,), (1,))
        )
        sens = sens - both[:width]
        state = state + both[width:]
    sens = jnp.where(where_am_i() == 0, 0.0, sens)
    out[:width] = sens
    out[width:] = state - jnp.broadcast_to(times(nodes[...], sens), state.shape)
    out[width + 1 : width + 2] = nodes[...]
    final[...] = state[:1]
    kept[...] = nodes[...]


def in_order(held, parts):
    member = lax.rem(where_am_i(), QUAD)
    for k, part in enumerate(parts):
        held[jnp.bitwise_xor(member, k)] = part[...]


def follow(entry, mapping):
    width = mapping.shape[1]
    return times(entry, mapping[:width]) + mapping[width : width + 1]


def quad_body(own, by1, by2, by3, final, following, total, leaving, defect, held):
    width = own.shape[1]
    in_order(held, (own, by1, by2, by3))
    member = lax.rem(where_am_i(), QUAD)
    beside = held[lax.rem(member + 1, QUAD), width + 1 : width + 2]
    last = member == QUAD - 1
    defect[...] = final[...] - jnp.where(last, following[...], beside)
    first = where_am_i() < QUAD

    @pl.when(first)
    def _():
        state = held[0, width : width + 1]
        for k in range(1, QUAD):
            state = follow(state, held[k])
        leaving[...] = state
        total[...] = jnp.zeros_like(total)

    @pl.when(jnp.logical_not(first))
    def _():
        put_composed(total, held[0], held[1])
        put_composed(held.at[0], held[2], held[3])
        put_composed(total, total[...], held[0])
        leaving[...] = total[width : width + 1]


def is_upper():
    return lax.rem(lax.div(where_am_i(), QUAD), 2) == 1


def prefix_body(own, by1, by2, by3, far, after, prefix, held):
    in_order(held, (own, by1, by2, by3))
    member = lax.rem(where_am_i(), QUAD)
    prefix[...] = held[0]

    @pl.when(jnp.logical_and(is_upper(), where_am_i() >= 2 * QUAD))
    def _():
        put_composed(prefix, far[...], held[0])

    for k in range(1, QUAD):

        @pl.when(member >= k)
        def _():
            put_composed(prefix, prefix[...], held[k])


def follow_body(entry, mapping, out):
    out[...] = follow(entry[...], mapping[...])


def follow_two_body(entry, own, far, out):
    upper = is_upper()

    @pl.when(upper)
    def _():
        out[...] = follow(follow(entry[...], far[...]), own[...])

    @pl.when(jnp.logical_not(upper))
    def _():
        out[...] = follow(follow(entry[...], own[...]), far[...])


def last_body(targets, *refs):
    *arrived, mapping, out = refs
    octet = lax.div(where_am_i(), 2 * QUAD)
    entry = jnp.zeros_like(out)
    for target, row in zip(targets, arrived):
        here = octet == target
        if target == 0:
            here = jnp.logical_and(here, is_upper())
        entry = jnp.where(here, row[...], entry)
    out[...] = follow(entry, mapping[...])


def on_device(nodes, jac_inverse, loss_rates, rate_table, rate_index):
    steps, width, _ = jac_inverse.shape
    seg_count = lax.axis_size("seg")
    segments = lax.axis_size("grp") * seg_count
    inv_len = 1.0 / (steps * segments)
    src_scale = 0.25 / steps

    def swapped(array, by):
        return lax.ppermute(array, AXES, [(i, i ^ by) for i in range(segments)])

    other = swapped(rate_table, seg_count)
    shape = ((width + PAD, width), F32)
    line = ((1, width), F32)
    early = call(
        functools.partial(early_body, inv_len),
        [
            line, line, (jac_inverse.shape, F32), (rate_index.shape, jnp.int32),
            ((steps, width), F32), ((width, width), F32), ((PAD, width), F32),
        ],
        *(
            pltpu.with_memory_space_constraint(array, pltpu.HBM)
            for array in (nodes, loss_rates[None], jac_inverse, rate_table, rate_index)
        ),
        scratch=[pltpu.VMEM(rate_table.shape, F32), pltpu.SemaphoreType.DMA((6,))],
        raw=True,
    )
    mapped, final, kept = call(
        functools.partial(local_body, inv_len, src_scale),
        [shape, line, line], other, *early,
    )
    parts = [swapped(mapped, k) for k in range(1, QUAD)]
    ends = range(QUAD, segments, QUAD)
    following = lax.ppermute(kept, AXES, [(i, i - 1) for i in ends])
    held = pltpu.VMEM((QUAD, *shape[0]), F32)
    quad, leaving, defect = call(
        quad_body, [shape, line, line], mapped, *parts, final, following, scratch=[held]
    )
    size = 2 * QUAD
    octets = segments // size

    def moved(array, start, by, count):
        pairs = [(start + k, start + k + by) for k in range(count)]
        return lax.ppermute(array, AXES, pairs)

    row = swapped(leaving, QUAD)
    far = swapped(quad, QUAD)
    arrived = [(0, row)]
    (leaving,) = call(follow_body, [line], row, quad)
    row = moved(leaving, QUAD, size, QUAD) + moved(leaving, QUAD, QUAD, QUAD)
    arrived.append((1, row))
    for octet in range(1, octets - 1):
        (leaving,) = call(follow_two_body, [line], row, quad, far)
        if octet < octets - 2:
            row = swapped(leaving, (octet ^ (octet + 1)) * size)
        else:
            row = moved(leaving, octet * size, size, size)
        arrived.append((octet + 1, row))
    (prefix,) = call(prefix_body, [shape], mapped, *parts, far, leaving, scratch=[held])
    targets, rows = zip(*arrived)
    (update,) = call(functools.partial(last_body, targets), [line], *rows, prefix)
    return (update, defect)


def solution(mesh):
    return jax.shard_map(
        on_device,
        mesh=mesh,
        in_specs=(
            P(("grp", "seg"), None),
            P(("grp", "seg"), None, None),
            P(),
            P("grp", None),
            P(("grp", "seg"), None),
        ),
        out_specs=(P(("grp", "seg"), None), P(("grp", "seg"), None)),
        check_vma=False,
    )
```

profile of v0, /device:TPU:27, one launch (start us, length us, event | category | flops | bytes accessed | tf_op | source)
XLA Modules:
  0.0 43.9 jit_solution(7168976251660289618)
XLA Ops:
  0.6 0.7 %collective-permute-start = (f32[64,256]{1,0:T(8,128)}, f32[64,256]{1,0:T(8,128)S(1)}, u32[]{:S(2)}, u32[]{:S(2)}) collective-permute-start(f32[64,256]{1,0:T(8,128)} %own_in.1), channel_id=1, source_target_pairs={{0,16},{1,17},{2,18},{3,19},{4,20},{5,21},{6,22},{7,23},{8,24},{9,... | collective-permute-start | bytes 196616 | tf_op jit(solution)/shard_map/ppermute | solution.py:234
  1.4 1.4 %shard_map.68 = (f32[1,256]{1,0:T(1,128)S(1)}, f32[1,256]{1,0:T(1,128)S(1)}, f32[4,256,256]{2,1,0:T(8,128)S(1)}, s32[4,256]{1,0:T(4,128)S(1)}, f32[4,256]{1,0:T(...) custom-call(f32[1,256]{1,0:T(1,128)} %nodes_in.1, f32[1,256]{1,0:T(1,128)} %bitcast.1, f32[4,256,256]{2,1,0:T(8,128)} %jac_in.1, ...), custom_call_target="tpu_custom_call" | custom-call | tf_op jit(solution)/shard_map/pallas_call | solution.py:44
  2.8 1.2 %shard_map.69 = (f32[264,256]{1,0:T(8,128)S(1)}, f32[1,256]{1,0:T(1,128)S(1)}, f32[1,256]{1,0:T(1,128)S(1)}) custom-call(f32[64,256]{1,0:T(8,128)S(1)} %collective-permute-done.other, f32[1,256]{1,0:T(1,128)S(1)} %get-tuple-element.15.nodes, f32[1,256]{1,0:T(1,128)S(1)} %get-tuple-element.16.loss, f32[4,256,256]{2,1,0:T(8,128)S(1)} %get-tuple-element.17.jac, ...), custom_call_target="tpu_custom_call" | custom-call | tf_op jit(solution)/shard_map/pallas_call | solution.py:44
  4.0 1.3 %collective-permute-start.3 = (f32[264,256]{1,0:T(8,128)S(1)}, f32[264,256]{1,0:T(8,128)S(1)}, u32[]{:S(2)}, u32[]{:S(2)}) collective-permute-start(f32[264,256]{1,0:T(8,128)S(1)} %get-tuple-element.22.own), channel_id=1, source_target_pairs={{0,3},{1,2},{2,1},{3,0},{4,7},{5,6},{6,5},{7,4},{8,11},{9,10},{10,... | collective-permute-start | bytes 811016 | tf_op jit(solution)/shard_map/ppermute | solution.py:234
  5.3 0.2 collective-permute-start.2
  5.5 1.2 %collective-permute-start.1 = (f32[264,256]{1,0:T(8,128)S(1)}, f32[264,256]{1,0:T(8,128)S(1)}, u32[]{:S(2)}, u32[]{:S(2)}) collective-permute-start(f32[264,256]{1,0:T(8,128)S(1)} %get-tuple-element.22.own), channel_id=1, source_target_pairs={{0,1},{1,0},{2,3},{3,2},{4,5},{5,4},{6,7},{7,6},{8,9},{9,8},{10,11... | collective-permute-start | bytes 811016 | tf_op jit(solution)/shard_map/ppermute | solution.py:234
  6.7 0.6 %collective-permute-start.4 = (f32[1,256]{1,0:T(1,128)S(1)}, f32[1,256]{1,0:T(1,128)S(1)}, u32[]{:S(2)}, u32[]{:S(2)}) collective-permute-start(f32[1,256]{1,0:T(1,128)S(1)} %get-tuple-element.24), channel_id=1, source_target_pairs={{4,3},{8,7},{12,11},{16,15},{20,19},{24,23},{28,27}} | collective-permute-start | bytes 3080 | tf_op jit(solution)/shard_map/ppermute | solution.py:258
  7.4 5.6 %collective-permute-done.3.by3 = f32[264,256]{1,0:T(8,128)S(1)} collective-permute-done((f32[264,256]{1,0:T(8,128)S(1)}, f32[264,256]{1,0:T(8,128)S(1)}, u32[]{:S(2)}, u32[]{:S(2)}) %collective-permute-start.3) | collective-permute-done | bytes 270368 | tf_op jit(solution)/shard_map/ppermute | solution.py:234
  13.0 6.2 %collective-permute-done.2.by2 = f32[264,256]{1,0:T(8,128)S(1)} collective-permute-done((f32[264,256]{1,0:T(8,128)S(1)}, f32[264,256]{1,0:T(8,128)S(1)}, u32[]{:S(2)}, u32[]{:S(2)}) %collective-permute-start.2) | collective-permute-done | bytes 270368 | tf_op jit(solution)/shard_map/ppermute | solution.py:234
  19.2 1.5 %shard_map.70 = (f32[264,256]{1,0:T(8,128)S(1)}, f32[1,256]{1,0:T(1,128)S(1)}, f32[1,256]{1,0:T(1,128)}) custom-call(f32[264,256]{1,0:T(8,128)S(1)} %get-tuple-element.22.own, f32[264,256]{1,0:T(8,128)S(1)} %collective-permute-done.1.by1, f32[264,256]{1,0:T(8,128)S(1)} %collective-permute-done.2.by2, f32[264,256]{1,0:T(8,128)S(1)} %collective-permute-done.3.by3, ...), custom_call_target="tpu_custom_call" | custom-call | tf_op jit(solution)/shard_map/pallas_call | solution.py:44
  20.7 0.2 collective-permute-start.8
  20.8 1.3 %collective-permute-start.5 = (f32[1,256]{1,0:T(1,128)S(1)}, f32[1,256]{1,0:T(1,128)S(1)}, u32[]{:S(2)}, u32[]{:S(2)}) collective-permute-start(f32[1,256]{1,0:T(1,128)S(1)} %get-tuple-element.25), channel_id=1, source_target_pairs={{0,4},{1,5},{2,6},{3,7},{4,0},{5,1},{6,2},{7,3},{8,12},{9,13},{10,... | collective-permute-start | bytes 3080 | tf_op jit(solution)/shard_map/ppermute | solution.py:234
  22.1 6.0 %collective-permute-done.5.entry.refs_0_ = f32[1,256]{1,0:T(1,128)S(1)} collective-permute-done((f32[1,256]{1,0:T(1,128)S(1)}, f32[1,256]{1,0:T(1,128)S(1)}, u32[]{:S(2)}, u32[]{:S(2)}) %collective-permute-start.5) | collective-permute-done | bytes 1056 | tf_op jit(solution)/shard_map/ppermute | solution.py:234
  28.2 0.1 shard_map.71
  28.3 0.7 %collective-permute-start.7 = (f32[1,256]{1,0:T(1,128)S(1)}, f32[1,256]{1,0:T(1,128)S(1)}, u32[]{:S(2)}, u32[]{:S(2)}) collective-permute-start(f32[1,256]{1,0:T(1,128)S(1)} %shard_map.71), channel_id=1, source_target_pairs={{4,8},{5,9},{6,10},{7,11}} | collective-permute-start | bytes 3080 | tf_op jit(solution)/shard_map/ppermute | solution.py:268
  29.0 0.7 %collective-permute-start.6 = (f32[1,256]{1,0:T(1,128)S(1)}, f32[1,256]{1,0:T(1,128)S(1)}, u32[]{:S(2)}, u32[]{:S(2)}) collective-permute-start(f32[1,256]{1,0:T(1,128)S(1)} %shard_map.71), channel_id=1, source_target_pairs={{4,12},{5,13},{6,14},{7,15}} | collective-permute-start | bytes 3080 | tf_op jit(solution)/shard_map/ppermute | solution.py:268
  29.7 0.3 shard_map.72
  29.9 6.5 %collective-permute-start.9 = (f32[1,256]{1,0:T(1,128)S(1)}, f32[1,256]{1,0:T(1,128)S(1)}, u32[]{:S(2)}, u32[]{:S(2)}) collective-permute-start(f32[1,256]{1,0:T(1,128)S(1)} %shard_map.72), channel_id=1, source_target_pairs={{0,24},{1,25},{2,26},{3,27},{4,28},{5,29},{6,30},{7,31},{8,16},{9,... | collective-permute-start | bytes 3080 | tf_op jit(solution)/shard_map/ppermute | solution.py:234
  36.5 1.3 %collective-permute-done.9.entry.refs_2_ = f32[1,256]{1,0:T(1,128)S(1)} collective-permute-done((f32[1,256]{1,0:T(1,128)S(1)}, f32[1,256]{1,0:T(1,128)S(1)}, u32[]{:S(2)}, u32[]{:S(2)}) %collective-permute-start.9) | collective-permute-done | bytes 1056 | tf_op jit(solution)/shard_map/ppermute | solution.py:234
  37.7 0.2 shard_map.73.after
  38.0 1.3 %collective-permute-start.10 = (f32[1,256]{1,0:T(1,128)S(1)}, f32[1,256]{1,0:T(1,128)S(1)}, u32[]{:S(2)}, u32[]{:S(2)}) collective-permute-start(f32[1,256]{1,0:T(1,128)S(1)} %shard_map.73.after), channel_id=1, source_target_pairs={{16,24},{17,25},{18,26},{19,27},{20,28},{21,29},{22,30},{23,31}} | collective-permute-start | bytes 3080 | tf_op jit(solution)/shard_map/ppermute | solution.py:268
  39.3 0.7 %shard_map.74.refs_4_ = f32[264,256]{1,0:T(8,128)S(1)} custom-call(f32[264,256]{1,0:T(8,128)S(1)} %get-tuple-element.22.own, f32[264,256]{1,0:T(8,128)S(1)} %collective-permute-done.1.by1, f32[264,256]{1,0:T(8,128)S(1)} %collective-permute-done.2.by2, f32[264,256]{1,0:T(8,128)S(1)} %collective-permute-done.3.by3, f32[264,256]{1,0:T(8,128)S(1)} %collective-permute-done.8.far, ...), custom_call_target="tpu_custom_call" | custom-call | tf_op jit(solution)/shard_map/pallas_call | solution.py:44
  40.0 3.2 %collective-permute-done.10.refs_3_ = f32[1,256]{1,0:T(1,128)S(1)} collective-permute-done((f32[1,256]{1,0:T(1,128)S(1)}, f32[1,256]{1,0:T(1,128)S(1)}, u32[]{:S(2)}, u32[]{:S(2)}) %collective-permute-start.10) | collective-permute-done | bytes 1056 | tf_op jit(solution)/shard_map/ppermute | solution.py:268
  43.2 0.7 %shard_map.75 = f32[1,256]{1,0:T(1,128)} custom-call(f32[1,256]{1,0:T(1,128)S(1)} %collective-permute-done.5.entry.refs_0_, f32[1,256]{1,0:T(1,128)S(1)} %add.3.entry.refs_1_, f32[1,256]{1,0:T(1,128)S(1)} %collective-permute-done.9.entry.refs_2_, f32[1,256]{1,0:T(1,128)S(1)} %collective-permute-done.10.refs_3_, f32[264,256]{1,0:T(8,128)S(1)} %shard_map.74.refs_4_), custom_call_target="tpu_custom_call" | custom-call | tf_op jit(solution)/shard_map/pallas_call | solution.py:44
  (7 shorter events, 0.0 us)
Async XLA Ops:
  0.6 2.2 %collective-permute-start = (f32[64,256]{1,0:T(8,128)}, f32[64,256]{1,0:T(8,128)S(1)}, u32[]{:S(2)}, u32[]{:S(2)}) collective-permute-start(f32[64,256]{1,0:T(8,128)} %own_in.1), channel_id=1, source_target_pairs={{0,16},{1,17},{2,18},{3,19},{4,20},{5,21},{6,22},{7,23},{8,24},{9,... | collective-permute-start | bytes 196616 | tf_op jit(solution)/shard_map/ppermute | solution.py:234
  4.0 9.0 %collective-permute-start.3 = (f32[264,256]{1,0:T(8,128)S(1)}, f32[264,256]{1,0:T(8,128)S(1)}, u32[]{:S(2)}, u32[]{:S(2)}) collective-permute-start(f32[264,256]{1,0:T(8,128)S(1)} %get-tuple-element.22.own), channel_id=1, source_target_pairs={{0,3},{1,2},{2,1},{3,0},{4,7},{5,6},{6,5},{7,4},{8,11},{9,10},{10,... | collective-permute-start | bytes 811016 | tf_op jit(solution)/shard_map/ppermute | solution.py:234
  5.3 13.9 %collective-permute-start.2 = (f32[264,256]{1,0:T(8,128)S(1)}, f32[264,256]{1,0:T(8,128)S(1)}, u32[]{:S(2)}, u32[]{:S(2)}) collective-permute-start(f32[264,256]{1,0:T(8,128)S(1)} %get-tuple-element.22.own), channel_id=1, source_target_pairs={{0,2},{1,3},{2,0},{3,1},{4,6},{5,7},{6,4},{7,5},{8,10},{9,11},{10,... | collective-permute-start | bytes 811016 | tf_op jit(solution)/shard_map/ppermute | solution.py:234
  5.5 13.7 %collective-permute-start.1 = (f32[264,256]{1,0:T(8,128)S(1)}, f32[264,256]{1,0:T(8,128)S(1)}, u32[]{:S(2)}, u32[]{:S(2)}) collective-permute-start(f32[264,256]{1,0:T(8,128)S(1)} %get-tuple-element.22.own), channel_id=1, source_target_pairs={{0,1},{1,0},{2,3},{3,2},{4,5},{5,4},{6,7},{7,6},{8,9},{9,8},{10,11... | collective-permute-start | bytes 811016 | tf_op jit(solution)/shard_map/ppermute | solution.py:234
  6.7 0.7 %collective-permute-start.4 = (f32[1,256]{1,0:T(1,128)S(1)}, f32[1,256]{1,0:T(1,128)S(1)}, u32[]{:S(2)}, u32[]{:S(2)}) collective-permute-start(f32[1,256]{1,0:T(1,128)S(1)} %get-tuple-element.24), channel_id=1, source_target_pairs={{4,3},{8,7},{12,11},{16,15},{20,19},{24,23},{28,27}} | collective-permute-start | bytes 3080 | tf_op jit(solution)/shard_map/ppermute | solution.py:258
  20.7 9.0 %collective-permute-start.8 = (f32[264,256]{1,0:T(8,128)S(1)}, f32[264,256]{1,0:T(8,128)S(1)}, u32[]{:S(2)}, u32[]{:S(2)}) collective-permute-start(f32[264,256]{1,0:T(8,128)S(1)} %get-tuple-element.26.mapping.own), channel_id=1, source_target_pairs={{0,4},{1,5},{2,6},{3,7},{4,0},{5,1},{6,2},{7,3},{8,12},{9,13},{10,... | collective-permute-start | bytes 811016 | tf_op jit(solution)/shard_map/ppermute | solution.py:234
  20.8 7.3 %collective-permute-start.5 = (f32[1,256]{1,0:T(1,128)S(1)}, f32[1,256]{1,0:T(1,128)S(1)}, u32[]{:S(2)}, u32[]{:S(2)}) collective-permute-start(f32[1,256]{1,0:T(1,128)S(1)} %get-tuple-element.25), channel_id=1, source_target_pairs={{0,4},{1,5},{2,6},{3,7},{4,0},{5,1},{6,2},{7,3},{8,12},{9,13},{10,... | collective-permute-start | bytes 3080 | tf_op jit(solution)/shard_map/ppermute | solution.py:234
  28.3 1.3 %collective-permute-start.7 = (f32[1,256]{1,0:T(1,128)S(1)}, f32[1,256]{1,0:T(1,128)S(1)}, u32[]{:S(2)}, u32[]{:S(2)}) collective-permute-start(f32[1,256]{1,0:T(1,128)S(1)} %shard_map.71), channel_id=1, source_target_pairs={{4,8},{5,9},{6,10},{7,11}} | collective-permute-start | bytes 3080 | tf_op jit(solution)/shard_map/ppermute | solution.py:268
  29.0 0.7 %collective-permute-start.6 = (f32[1,256]{1,0:T(1,128)S(1)}, f32[1,256]{1,0:T(1,128)S(1)}, u32[]{:S(2)}, u32[]{:S(2)}) collective-permute-start(f32[1,256]{1,0:T(1,128)S(1)} %shard_map.71), channel_id=1, source_target_pairs={{4,12},{5,13},{6,14},{7,15}} | collective-permute-start | bytes 3080 | tf_op jit(solution)/shard_map/ppermute | solution.py:268
  29.9 7.8 %collective-permute-start.9 = (f32[1,256]{1,0:T(1,128)S(1)}, f32[1,256]{1,0:T(1,128)S(1)}, u32[]{:S(2)}, u32[]{:S(2)}) collective-permute-start(f32[1,256]{1,0:T(1,128)S(1)} %shard_map.72), channel_id=1, source_target_pairs={{0,24},{1,25},{2,26},{3,27},{4,28},{5,29},{6,30},{7,31},{8,16},{9,... | collective-permute-start | bytes 3080 | tf_op jit(solution)/shard_map/ppermute | solution.py:234
  38.0 5.2 %collective-permute-start.10 = (f32[1,256]{1,0:T(1,128)S(1)}, f32[1,256]{1,0:T(1,128)S(1)}, u32[]{:S(2)}, u32[]{:S(2)}) collective-permute-start(f32[1,256]{1,0:T(1,128)S(1)} %shard_map.73.after), channel_id=1, source_target_pairs={{16,24},{17,25},{18,26},{19,27},{20,28},{21,29},{22,30},{23,31}} | collective-permute-start | bytes 3080 | tf_op jit(solution)/shard_map/ppermute | solution.py:268
where the time goes:
time: 44.1 us; the launch traced here: 43.9 us
  waiting for transfers between devices  22.3 us (51%)
  starting transfers between devices  14.7 us (33%)
  Pallas kernels  6.1 us (14%)
  between operations  0.76 us (2%)
    ppermute x7, waiting for transfers between devices, swapped(): return lax.ppermute(array, AXES, [(i, i ^ by) for i in range(segments)])  19.1 us
    ppermute x7, starting transfers between devices, swapped(): return lax.ppermute(array, AXES, [(i, i ^ by) for i in range(segments)])  11.5 us
    pallas_call x8, Pallas kernels, call(): pl.pallas_call(body, out_shape=out, in_specs=[HBM if raw else VMEM] * len...  6.1 us
    ppermute x3, waiting for transfers between devices, moved(): return lax.ppermute(array, AXES, pairs)  3.23 us
    ppermute x3, starting transfers between devices, moved(): return lax.ppermute(array, AXES, pairs)  2.62 us
  transfers between devices with their start and end apart: 11, of which 5 were waited for; matrix products, arithmetic and copies ran while one was open for 0% of the time, Pallas kernels for 5%

commit v1 on v0

--- a/solution.py
+++ b/solution.py
@@ -110,9 +110,10 @@
 
 def local_body(
     inv_len, src_scale, other, nodes, loss, jac, index, near, sens_in, state_in,
-    out, final, kept,
+    top, bottom, final,
 ):
     steps, width, _ = jac.shape
+    cut = top.shape[0]
     rows = other.shape[0]
     source = near[...] + lookup(other, index, (1 - lax.axis_index("grp")) * rows)
     rates = loss[...]
@@ -132,17 +133,21 @@
         sens = sens - both[:width]
         state = state + both[width:]
     sens = jnp.where(where_am_i() == 0, 0.0, sens)
-    out[:width] = sens
-    out[width:] = state - jnp.broadcast_to(times(nodes[...], sens), state.shape)
-    out[width + 1 : width + 2] = nodes[...]
+    top[...] = sens[:cut]
+    bottom[: width - cut] = sens[cut:]
+    offset = state - jnp.broadcast_to(times(nodes[...], sens), state.shape)
+    bottom[width - cut :] = offset
+    bottom[width - cut + 1 : width - cut + 2] = nodes[...]
     final[...] = state[:1]
-    kept[...] = nodes[...]
 
 
 def in_order(held, parts):
     member = lax.rem(where_am_i(), QUAD)
-    for k, part in enumerate(parts):
-        held[jnp.bitwise_xor(member, k)] = part[...]
+    cut = parts[0].shape[0]
+    for k in range(QUAD):
+        place = jnp.bitwise_xor(member, k)
+        held[place, :cut] = parts[2 * k][...]
+        held[place, cut:] = parts[2 * k + 1][...]
 
 
 def follow(entry, mapping):
@@ -150,37 +155,62 @@
     return times(entry, mapping[:width]) + mapping[width : width + 1]
 
 
-def quad_body(own, by1, by2, by3, final, following, total, leaving, defect, held):
-    width = own.shape[1]
-    in_order(held, (own, by1, by2, by3))
+def first_exit_body(*refs):
+    *parts, leaving = refs
+    place = where_am_i()
+    width = leaving.shape[1]
+    cut = parts[0].shape[0]
+
+    def step(state, k):
+        upper, lower = parts[2 * k : 2 * k + 2]
+        rest = width - cut
+        n = lax.broadcasted_iota(jnp.int32, (width, width), 0)
+        on = n == lax.broadcasted_iota(jnp.int32, (width, width), 1)
+        column = jnp.sum(jnp.where(on, state, 0.0), axis=1, keepdims=True)
+        return (
+            jnp.sum(upper[...] * column[:cut], axis=0, keepdims=True)
+            + jnp.sum(lower[:rest] * column[cut:], axis=0, keepdims=True)
+            + lower[rest : rest + 1]
+        )
+
+    for member in range(QUAD):
+
+        @pl.when(place == member)
+        def _():
+            state = parts[2 * member + 1][width - cut : width - cut + 1]
+            for k in range(1, QUAD):
+                state = step(state, member ^ k)
+            leaving[...] = state
+
+
+def quad_body(*refs):
+    *parts, after, total, beside, held = refs
+    width = total.shape[1]
+    in_order(held, parts)
     member = lax.rem(where_am_i(), QUAD)
-    beside = held[lax.rem(member + 1, QUAD), width + 1 : width + 2]
-    last = member == QUAD - 1
-    defect[...] = final[...] - jnp.where(last, following[...], beside)
-    first = where_am_i() < QUAD
-
-    @pl.when(first)
-    def _():
-        state = held[0, width : width + 1]
-        for k in range(1, QUAD):
-            state = follow(state, held[k])
-        leaving[...] = state
+    node = width + 1
+    beside[...] = held[lax.rem(member + 1, QUAD), node : node + 1]
+
+    @pl.when(where_am_i() < QUAD)
+    def _():
         total[...] = jnp.zeros_like(total)
 
-    @pl.when(jnp.logical_not(first))
-    def _():
+    @pl.when(where_am_i() >= QUAD)
+    def _():
+        head = held[0, node : node + 1]
         put_composed(total, held[0], held[1])
         put_composed(held.at[0], held[2], held[3])
         put_composed(total, total[...], held[0])
-        leaving[...] = total[width : width + 1]
+        total[node : node + 1] = head
 
 
 def is_upper():
     return lax.rem(lax.div(where_am_i(), QUAD), 2) == 1
 
 
-def prefix_body(own, by1, by2, by3, far, after, prefix, held):
-    in_order(held, (own, by1, by2, by3))
+def prefix_body(*refs):
+    *parts, far, after, prefix, held = refs
+    in_order(held, parts)
     member = lax.rem(where_am_i(), QUAD)
     prefix[...] = held[0]
 
@@ -199,28 +229,43 @@
     out[...] = follow(entry[...], mapping[...])
 
 
-def follow_two_body(entry, own, far, out):
+def octet_exit_body(entry, own, far, out):
     upper = is_upper()
+    width = own.shape[1]
+    at = entry[:1]
 
     @pl.when(upper)
     def _():
-        out[...] = follow(follow(entry[...], far[...]), own[...])
+        out[:1] = follow(follow(at, far[...]), own[...])
+        out[1:2] = far[width + 1 : width + 2]
 
     @pl.when(jnp.logical_not(upper))
     def _():
-        out[...] = follow(follow(entry[...], own[...]), far[...])
-
-
-def last_body(targets, *refs):
-    *arrived, mapping, out = refs
-    octet = lax.div(where_am_i(), 2 * QUAD)
+        out[:1] = follow(follow(at, own[...]), far[...])
+        out[1:2] = own[width + 1 : width + 2]
+
+    out[2:] = jnp.zeros_like(out[2:])
+
+
+def last_body(targets, sources, *refs):
+    *arrived, final, beside, far, back, mapping, out, defect = refs
+    place = where_am_i()
+    width = out.shape[1]
+    member = lax.rem(place, QUAD)
+    octet = lax.div(place, 2 * QUAD)
     entry = jnp.zeros_like(out)
+    following = jnp.where(member == QUAD - 1, far[width + 1 : width + 2], beside[...])
+    following = jnp.where(is_upper() & (member == QUAD - 1), back[...], following)
     for target, row in zip(targets, arrived):
         here = octet == target
         if target == 0:
             here = jnp.logical_and(here, is_upper())
-        entry = jnp.where(here, row[...], entry)
+        entry = jnp.where(here, row[:1], entry)
+    for source, k in sources:
+        ends = place == 2 * QUAD * (source + 1) - 1
+        following = jnp.where(ends, arrived[k][1:2], following)
     out[...] = follow(entry, mapping[...])
+    defect[...] = final[...] - following
 
 
 def on_device(nodes, jac_inverse, loss_rates, rate_table, rate_index):
@@ -249,17 +294,20 @@
         scratch=[pltpu.VMEM(rate_table.shape, F32), pltpu.SemaphoreType.DMA((6,))],
         raw=True,
     )
-    mapped, final, kept = call(
+    cut = width // 2
+    halves = [((cut, width), F32), ((width - cut + PAD, width), F32)]
+    top, bottom, final = call(
         functools.partial(local_body, inv_len, src_scale),
-        [shape, line, line], other, *early,
-    )
-    parts = [swapped(mapped, k) for k in range(1, QUAD)]
-    ends = range(QUAD, segments, QUAD)
-    following = lax.ppermute(kept, AXES, [(i, i - 1) for i in ends])
-    held = pltpu.VMEM((QUAD, *shape[0]), F32)
-    quad, leaving, defect = call(
-        quad_body, [shape, line, line], mapped, *parts, final, following, scratch=[held]
-    )
+        [*halves, line], other, *early,
+    )
+    top1 = swapped(top, 1)
+    bottom2 = swapped(bottom, 2)
+    bottom1 = swapped(bottom, 1)
+    top2 = swapped(top, 2)
+    top3 = swapped(top1, 2)
+    bottom3 = swapped(bottom2, 1)
+    parts = [top, bottom, top1, bottom1, top2, bottom2, top3, bottom3]
+    (leaving,) = call(first_exit_body, [line], *parts)
     size = 2 * QUAD
     octets = segments // size
 
@@ -268,22 +316,33 @@
         return lax.ppermute(array, AXES, pairs)
 
     row = swapped(leaving, QUAD)
+    held = pltpu.VMEM((QUAD, *shape[0]), F32)
+    quad, beside = call(quad_body, [shape, line], *parts, leaving, scratch=[held])
     far = swapped(quad, QUAD)
     arrived = [(0, row)]
     (leaving,) = call(follow_body, [line], row, quad)
-    row = moved(leaving, QUAD, size, QUAD) + moved(leaving, QUAD, QUAD, QUAD)
+    low = moved(leaving, QUAD, QUAD, QUAD)
+    high = moved(leaving, QUAD, size, QUAD)
+    row = high + low
     arrived.append((1, row))
+    end = (octets - 1) * size
+    last = moved(early[0], end, -1, 1)
+    sources = []
     for octet in range(1, octets - 1):
-        (leaving,) = call(follow_two_body, [line], row, quad, far)
-        if octet < octets - 2:
+        (leaving,) = call(octet_exit_body, [((PAD, width), F32)], row, quad, far)
+        if octet == octets - 2:
+            row = moved(leaving, octet * size, size, size)
+        else:
+            sources.append((octet, len(arrived)))
             row = swapped(leaving, (octet ^ (octet + 1)) * size)
-        else:
-            row = moved(leaving, octet * size, size, size)
         arrived.append((octet + 1, row))
-    (prefix,) = call(prefix_body, [shape], mapped, *parts, far, leaving, scratch=[held])
+    first = moved(early[0], size, -1, 1)
+    (prefix,) = call(prefix_body, [shape], *parts, far, leaving, scratch=[held])
     targets, rows = zip(*arrived)
-    (update,) = call(functools.partial(last_body, targets), [line], *rows, prefix)
-    return (update, defect)
+    return call(
+        functools.partial(last_body, targets, sources),
+        [line, line], *rows, final, beside, far, first + last, prefix,
+    )
 
 
 def solution(mesh):

time: 44.1 us -> 47.1 us (1.068)
  the two profiles are of different devices: /device:TPU:27 before, /device:TPU:15 now
where the time goes in v1:
time: 47.1 us; the launch traced here: 46.9 us
  starting transfers between devices  21.2 us (45%)
  waiting for transfers between devices  18.8 us (40%)
  Pallas kernels  6.09 us (13%)
  between operations  0.77 us (2%)
    ppermute x10, starting transfers between devices, swapped(): return lax.ppermute(array, AXES, [(i, i ^ by) for i in range(segments)])  16.6 us
    ppermute x10, waiting for transfers between devices, swapped(): return lax.ppermute(array, AXES, [(i, i ^ by) for i in range(segments)])  14.6 us
    pallas_call x9, Pallas kernels, call(): pl.pallas_call(body, out_shape=out, in_specs=[HBM if raw else VMEM] * len...  6.09 us
    ppermute x5, starting transfers between devices, moved(): return lax.ppermute(array, AXES, pairs)  4.65 us
    ppermute x5, waiting for transfers between devices, moved(): return lax.ppermute(array, AXES, pairs)  4.16 us
  transfers between devices with their start and end apart: 15, of which 6 were waited for; matrix products, arithmetic and copies ran while one was open for 0% of the time, Pallas kernels for 6%

profile of v1, /device:TPU:15, one launch (start us, length us, event | category | flops | bytes accessed | tf_op | source)
XLA Modules:
  0.0 46.9 jit_solution(2416318572755438193)
XLA Ops:
  0.6 0.7 %collective-permute-start = (f32[64,256]{1,0:T(8,128)}, f32[64,256]{1,0:T(8,128)S(1)}, u32[]{:S(2)}, u32[]{:S(2)}) collective-permute-start(f32[64,256]{1,0:T(8,128)} %own_in.1), channel_id=1, source_target_pairs={{0,16},{1,17},{2,18},{3,19},{4,20},{5,21},{6,22},{7,23},{8,24},{9,... | collective-permute-start | bytes 196616 | tf_op jit(solution)/shard_map/ppermute | solution.py:279
  1.4 1.4 %shard_map.68 = (f32[1,256]{1,0:T(1,128)S(1)}, f32[1,256]{1,0:T(1,128)S(1)}, f32[4,256,256]{2,1,0:T(8,128)S(1)}, s32[4,256]{1,0:T(4,128)S(1)}, f32[4,256]{1,0:T(...) custom-call(f32[1,256]{1,0:T(1,128)} %nodes_in.1, f32[1,256]{1,0:T(1,128)} %bitcast.1, f32[4,256,256]{2,1,0:T(8,128)} %jac_in.1, ...), custom_call_target="tpu_custom_call" | custom-call | tf_op jit(solution)/shard_map/pallas_call | solution.py:44
  2.8 1.2 %shard_map.69 = (f32[128,256]{1,0:T(8,128)S(1)}, f32[136,256]{1,0:T(8,128)S(1)}, f32[1,256]{1,0:T(1,128)S(1)}) custom-call(f32[64,256]{1,0:T(8,128)S(1)} %collective-permute-done.other, f32[1,256]{1,0:T(1,128)S(1)} %get-tuple-element.14.nodes, f32[1,256]{1,0:T(1,128)S(1)} %get-tuple-element.15.loss, f32[4,256,256]{2,1,0:T(8,128)S(1)} %get-tuple-element.16.jac, ...), custom_call_target="tpu_custom_call" | custom-call | tf_op jit(solution)/shard_map/pallas_call | solution.py:44
  4.0 0.3 collective-permute-start.4
  4.3 0.3 collective-permute-start.1
  4.5 1.2 %collective-permute-start.2 = (f32[136,256]{1,0:T(8,128)S(1)}, f32[136,256]{1,0:T(8,128)S(1)}, u32[]{:S(2)}, u32[]{:S(2)}) collective-permute-start(f32[136,256]{1,0:T(8,128)S(1)} %get-tuple-element.22.refs_1_), channel_id=1, source_target_pairs={{0,1},{1,0},{2,3},{3,2},{4,5},{5,4},{6,7},{7,6},{8,9},{9,8},{10,11... | collective-permute-start | bytes 417800 | tf_op jit(solution)/shard_map/ppermute | solution.py:279
  5.8 3.5 %collective-permute-done.4.refs_5_ = f32[136,256]{1,0:T(8,128)S(1)} collective-permute-done((f32[136,256]{1,0:T(8,128)S(1)}, f32[136,256]{1,0:T(8,128)S(1)}, u32[]{:S(2)}, u32[]{:S(2)}) %collective-permute-start.4) | collective-permute-done | bytes 139296 | tf_op jit(solution)/shard_map/ppermute | solution.py:279
  9.7 1.2 %collective-permute-start.5 = (f32[128,256]{1,0:T(8,128)S(1)}, f32[128,256]{1,0:T(8,128)S(1)}, u32[]{:S(2)}, u32[]{:S(2)}) collective-permute-start(f32[128,256]{1,0:T(8,128)S(1)} %collective-permute-done.1.refs_2_), channel_id=1, source_target_pairs={{0,2},{1,3},{2,0},{3,1},{4,6},{5,7},{6,4},{7,5},{8,10},{9,11},{10,... | collective-permute-start | bytes 393224 | tf_op jit(solution)/shard_map/ppermute | solution.py:279
  11.0 2.6 %collective-permute-done.3.refs_4_ = f32[128,256]{1,0:T(8,128)S(1)} collective-permute-done((f32[128,256]{1,0:T(8,128)S(1)}, f32[128,256]{1,0:T(8,128)S(1)}, u32[]{:S(2)}, u32[]{:S(2)}) %collective-permute-start.3) | collective-permute-done | bytes 131104 | tf_op jit(solution)/shard_map/ppermute | solution.py:279
  13.6 2.6 %collective-permute-done.5.refs_6_ = f32[128,256]{1,0:T(8,128)S(1)} collective-permute-done((f32[128,256]{1,0:T(8,128)S(1)}, f32[128,256]{1,0:T(8,128)S(1)}, u32[]{:S(2)}, u32[]{:S(2)}) %collective-permute-start.5) | collective-permute-done | bytes 131104 | tf_op jit(solution)/shard_map/ppermute | solution.py:279
  16.2 0.9 %shard_map.71 = (f32[264,256]{1,0:T(8,128)S(1)}, f32[1,256]{1,0:T(1,128)S(1)}) custom-call(f32[128,256]{1,0:T(8,128)S(1)} %get-tuple-element.21.refs_0_, f32[136,256]{1,0:T(8,128)S(1)} %get-tuple-element.22.refs_1_, f32[128,256]{1,0:T(8,128)S(1)} %collective-permute-done.1.refs_2_, f32[136,256]{1,0:T(8,128)S(1)} %collective-permute-done.2.refs_3_, ...), custom_call_target="tpu_custom_call" | custom-call | tf_op jit(solution)/shard_map/pallas_call | solution.py:44
  17.4 1.3 %collective-permute-start.7 = (f32[1,256]{1,0:T(1,128)S(1)}, f32[1,256]{1,0:T(1,128)S(1)}, u32[]{:S(2)}, u32[]{:S(2)}) collective-permute-start(f32[1,256]{1,0:T(1,128)S(1)} %shard_map.70.refs_8_), channel_id=1, source_target_pairs={{0,4},{1,5},{2,6},{3,7},{4,0},{5,1},{6,2},{7,3},{8,12},{9,13},{10,... | collective-permute-start | bytes 3080 | tf_op jit(solution)/shard_map/ppermute | solution.py:279
  18.7 4.6 %collective-permute-done.7.entry.refs_0_ = f32[1,256]{1,0:T(1,128)S(1)} collective-permute-done((f32[1,256]{1,0:T(1,128)S(1)}, f32[1,256]{1,0:T(1,128)S(1)}, u32[]{:S(2)}, u32[]{:S(2)}) %collective-permute-start.7) | collective-permute-done | bytes 1056 | tf_op jit(solution)/shard_map/ppermute | solution.py:279
  23.4 0.7 %collective-permute-start.9 = (f32[1,256]{1,0:T(1,128)S(1)}, f32[1,256]{1,0:T(1,128)S(1)}, u32[]{:S(2)}, u32[]{:S(2)}) collective-permute-start(f32[1,256]{1,0:T(1,128)S(1)} %shard_map.72), channel_id=1, source_target_pairs={{4,8},{5,9},{6,10},{7,11}} | collective-permute-start | bytes 3080 | tf_op jit(solution)/shard_map/ppermute | solution.py:316
  24.0 0.7 %collective-permute-start.8 = (f32[1,256]{1,0:T(1,128)S(1)}, f32[1,256]{1,0:T(1,128)S(1)}, u32[]{:S(2)}, u32[]{:S(2)}) collective-permute-start(f32[1,256]{1,0:T(1,128)S(1)} %shard_map.72), channel_id=1, source_target_pairs={{4,12},{5,13},{6,14},{7,15}} | collective-permute-start | bytes 3080 | tf_op jit(solution)/shard_map/ppermute | solution.py:316
  24.7 0.3 shard_map.73
  25.0 10.8 %collective-permute-start.11 = (f32[8,256]{1,0:T(8,128)S(1)}, f32[8,256]{1,0:T(8,128)S(1)}, u32[]{:S(2)}, u32[]{:S(2)}) collective-permute-start(f32[8,256]{1,0:T(8,128)S(1)} %shard_map.73), channel_id=1, source_target_pairs={{0,24},{1,25},{2,26},{3,27},{4,28},{5,29},{6,30},{7,31},{8,16},{9,... | collective-permute-start | bytes 24584 | tf_op jit(solution)/shard_map/ppermute | solution.py:279
  35.8 1.3 %collective-permute-done.11.entry.refs_2_ = f32[8,256]{1,0:T(8,128)S(1)} collective-permute-done((f32[8,256]{1,0:T(8,128)S(1)}, f32[8,256]{1,0:T(8,128)S(1)}, u32[]{:S(2)}, u32[]{:S(2)}) %collective-permute-start.11) | collective-permute-done | bytes 8224 | tf_op jit(solution)/shard_map/ppermute | solution.py:279
  37.4 1.4 %collective-permute-start.12 = (f32[8,256]{1,0:T(8,128)S(1)}, f32[8,256]{1,0:T(8,128)S(1)}, u32[]{:S(2)}, u32[]{:S(2)}) collective-permute-start(f32[8,256]{1,0:T(8,128)S(1)} %shard_map.74.refs_9_), channel_id=1, source_target_pairs={{16,24},{17,25},{18,26},{19,27},{20,28},{21,29},{22,30},{23,31}} | collective-permute-start | bytes 24584 | tf_op jit(solution)/shard_map/ppermute | solution.py:316
  38.8 1.3 %collective-permute-start.14 = (f32[1,256]{1,0:T(1,128)S(1)}, f32[1,256]{1,0:T(1,128)S(1)}, u32[]{:S(2)}, u32[]{:S(2)}) collective-permute-start(f32[1,256]{1,0:T(1,128)S(1)} %get-tuple-element.14.nodes), channel_id=1, source_target_pairs={{24,23}} | collective-permute-start | bytes 3080 | tf_op jit(solution)/shard_map/ppermute | solution.py:316
  40.1 0.7 %collective-permute-start.13 = (f32[1,256]{1,0:T(1,128)S(1)}, f32[1,256]{1,0:T(1,128)S(1)}, u32[]{:S(2)}, u32[]{:S(2)}) collective-permute-start(f32[1,256]{1,0:T(1,128)S(1)} %get-tuple-element.14.nodes), channel_id=1, source_target_pairs={{8,7}} | collective-permute-start | bytes 3080 | tf_op jit(solution)/shard_map/ppermute | solution.py:316
  40.8 4.1 %collective-permute-done.14 = f32[1,256]{1,0:T(1,128)S(1)} collective-permute-done((f32[1,256]{1,0:T(1,128)S(1)}, f32[1,256]{1,0:T(1,128)S(1)}, u32[]{:S(2)}, u32[]{:S(2)}) %collective-permute-start.14) | collective-permute-done | bytes 1056 | tf_op jit(solution)/shard_map/ppermute | solution.py:316
  44.9 1.2 %shard_map.75.refs_8_ = f32[264,256]{1,0:T(8,128)S(1)} custom-call(f32[128,256]{1,0:T(8,128)S(1)} %get-tuple-element.21.refs_0_, f32[136,256]{1,0:T(8,128)S(1)} %get-tuple-element.22.refs_1_, f32[128,256]{1,0:T(8,128)S(1)} %collective-permute-done.1.refs_2_, f32[136,256]{1,0:T(8,128)S(1)} %collective-permute-done.2.refs_3_, ...), custom_call_target="tpu_custom_call" | custom-call | tf_op jit(solution)/shard_map/pallas_call | solution.py:44
  46.2 0.7 %shard_map.76 = (f32[1,256]{1,0:T(1,128)}, f32[1,256]{1,0:T(1,128)}) custom-call(f32[1,256]{1,0:T(1,128)S(1)} %collective-permute-done.7.entry.refs_0_, f32[1,256]{1,0:T(1,128)S(1)} %add.6.entry.refs_1_, f32[8,256]{1,0:T(8,128)S(1)} %collective-permute-done.11.entry.refs_2_, f32[8,256]{1,0:T(8,128)S(1)} %collective-permute-done.12.refs_3_, ...), custom_call_target="tpu_custom_call" | custom-call | tf_op jit(solution)/shard_map/pallas_call | solution.py:44
  (17 shorter events, 1.1 us)
Async XLA Ops:
  0.6 2.2 %collective-permute-start = (f32[64,256]{1,0:T(8,128)}, f32[64,256]{1,0:T(8,128)S(1)}, u32[]{:S(2)}, u32[]{:S(2)}) collective-permute-start(f32[64,256]{1,0:T(8,128)} %own_in.1), channel_id=1, source_target_pairs={{0,16},{1,17},{2,18},{3,19},{4,20},{5,21},{6,22},{7,23},{8,24},{9,... | collective-permute-start | bytes 196616 | tf_op jit(solution)/shard_map/ppermute | solution.py:279
  4.0 5.3 %collective-permute-start.4 = (f32[136,256]{1,0:T(8,128)S(1)}, f32[136,256]{1,0:T(8,128)S(1)}, u32[]{:S(2)}, u32[]{:S(2)}) collective-permute-start(f32[136,256]{1,0:T(8,128)S(1)} %get-tuple-element.22.refs_1_), channel_id=1, source_target_pairs={{0,2},{1,3},{2,0},{3,1},{4,6},{5,7},{6,4},{7,5},{8,10},{9,11},{10,... | collective-permute-start | bytes 417800 | tf_op jit(solution)/shard_map/ppermute | solution.py:279
  4.3 5.5 %collective-permute-start.1 = (f32[128,256]{1,0:T(8,128)S(1)}, f32[128,256]{1,0:T(8,128)S(1)}, u32[]{:S(2)}, u32[]{:S(2)}) collective-permute-start(f32[128,256]{1,0:T(8,128)S(1)} %get-tuple-element.21.refs_0_), channel_id=1, source_target_pairs={{0,1},{1,0},{2,3},{3,2},{4,5},{5,4},{6,7},{7,6},{8,9},{9,8},{10,11... | collective-permute-start | bytes 393224 | tf_op jit(solution)/shard_map/ppermute | solution.py:279
  4.5 9.1 %collective-permute-start.2 = (f32[136,256]{1,0:T(8,128)S(1)}, f32[136,256]{1,0:T(8,128)S(1)}, u32[]{:S(2)}, u32[]{:S(2)}) collective-permute-start(f32[136,256]{1,0:T(8,128)S(1)} %get-tuple-element.22.refs_1_), channel_id=1, source_target_pairs={{0,1},{1,0},{2,3},{3,2},{4,5},{5,4},{6,7},{7,6},{8,9},{9,8},{10,11... | collective-permute-start | bytes 417800 | tf_op jit(solution)/shard_map/ppermute | solution.py:279
  9.3 6.9 %collective-permute-start.6 = (f32[136,256]{1,0:T(8,128)S(1)}, f32[136,256]{1,0:T(8,128)S(1)}, u32[]{:S(2)}, u32[]{:S(2)}) collective-permute-start(f32[136,256]{1,0:T(8,128)S(1)} %collective-permute-done.4.refs_5_), channel_id=1, source_target_pairs={{0,1},{1,0},{2,3},{3,2},{4,5},{5,4},{6,7},{7,6},{8,9},{9,8},{10,11... | collective-permute-start | bytes 417800 | tf_op jit(solution)/shard_map/ppermute | solution.py:279
  9.5 4.1 %collective-permute-start.3 = (f32[128,256]{1,0:T(8,128)S(1)}, f32[128,256]{1,0:T(8,128)S(1)}, u32[]{:S(2)}, u32[]{:S(2)}) collective-permute-start(f32[128,256]{1,0:T(8,128)S(1)} %get-tuple-element.21.refs_0_), channel_id=1, source_target_pairs={{0,2},{1,3},{2,0},{3,1},{4,6},{5,7},{6,4},{7,5},{8,10},{9,11},{10,... | collective-permute-start | bytes 393224 | tf_op jit(solution)/shard_map/ppermute | solution.py:279
  9.7 6.5 %collective-permute-start.5 = (f32[128,256]{1,0:T(8,128)S(1)}, f32[128,256]{1,0:T(8,128)S(1)}, u32[]{:S(2)}, u32[]{:S(2)}) collective-permute-start(f32[128,256]{1,0:T(8,128)S(1)} %collective-permute-done.1.refs_2_), channel_id=1, source_target_pairs={{0,2},{1,3},{2,0},{3,1},{4,6},{5,7},{6,4},{7,5},{8,10},{9,11},{10,... | collective-permute-start | bytes 393224 | tf_op jit(solution)/shard_map/ppermute | solution.py:279
  17.1 7.6 %collective-permute-start.10 = (f32[264,256]{1,0:T(8,128)S(1)}, f32[264,256]{1,0:T(8,128)S(1)}, u32[]{:S(2)}, u32[]{:S(2)}) collective-permute-start(f32[264,256]{1,0:T(8,128)S(1)} %get-tuple-element.23.mapping.own), channel_id=1, source_target_pairs={{0,4},{1,5},{2,6},{3,7},{4,0},{5,1},{6,2},{7,3},{8,12},{9,13},{10,... | collective-permute-start | bytes 811016 | tf_op jit(solution)/shard_map/ppermute | solution.py:279
  17.4 5.9 %collective-permute-start.7 = (f32[1,256]{1,0:T(1,128)S(1)}, f32[1,256]{1,0:T(1,128)S(1)}, u32[]{:S(2)}, u32[]{:S(2)}) collective-permute-start(f32[1,256]{1,0:T(1,128)S(1)} %shard_map.70.refs_8_), channel_id=1, source_target_pairs={{0,4},{1,5},{2,6},{3,7},{4,0},{5,1},{6,2},{7,3},{8,12},{9,13},{10,... | collective-permute-start | bytes 3080 | tf_op jit(solution)/shard_map/ppermute | solution.py:279
  23.4 1.3 %collective-permute-start.9 = (f32[1,256]{1,0:T(1,128)S(1)}, f32[1,256]{1,0:T(1,128)S(1)}, u32[]{:S(2)}, u32[]{:S(2)}) collective-permute-start(f32[1,256]{1,0:T(1,128)S(1)} %shard_map.72), channel_id=1, source_target_pairs={{4,8},{5,9},{6,10},{7,11}} | collective-permute-start | bytes 3080 | tf_op jit(solution)/shard_map/ppermute | solution.py:316
  24.0 0.7 %collective-permute-start.8 = (f32[1,256]{1,0:T(1,128)S(1)}, f32[1,256]{1,0:T(1,128)S(1)}, u32[]{:S(2)}, u32[]{:S(2)}) collective-permute-start(f32[1,256]{1,0:T(1,128)S(1)} %shard_map.72), channel_id=1, source_target_pairs={{4,12},{5,13},{6,14},{7,15}} | collective-permute-start | bytes 3080 | tf_op jit(solution)/shard_map/ppermute | solution.py:316
  25.0 12.2 %collective-permute-start.11 = (f32[8,256]{1,0:T(8,128)S(1)}, f32[8,256]{1,0:T(8,128)S(1)}, u32[]{:S(2)}, u32[]{:S(2)}) collective-permute-start(f32[8,256]{1,0:T(8,128)S(1)} %shard_map.73), channel_id=1, source_target_pairs={{0,24},{1,25},{2,26},{3,27},{4,28},{5,29},{6,30},{7,31},{8,16},{9,... | collective-permute-start | bytes 24584 | tf_op jit(solution)/shard_map/ppermute | solution.py:279
  37.4 8.8 %collective-permute-start.12 = (f32[8,256]{1,0:T(8,128)S(1)}, f32[8,256]{1,0:T(8,128)S(1)}, u32[]{:S(2)}, u32[]{:S(2)}) collective-permute-start(f32[8,256]{1,0:T(8,128)S(1)} %shard_map.74.refs_9_), channel_id=1, source_target_pairs={{16,24},{17,25},{18,26},{19,27},{20,28},{21,29},{22,30},{23,31}} | collective-permute-start | bytes 24584 | tf_op jit(solution)/shard_map/ppermute | solution.py:316
  38.8 6.1 %collective-permute-start.14 = (f32[1,256]{1,0:T(1,128)S(1)}, f32[1,256]{1,0:T(1,128)S(1)}, u32[]{:S(2)}, u32[]{:S(2)}) collective-permute-start(f32[1,256]{1,0:T(1,128)S(1)} %get-tuple-element.14.nodes), channel_id=1, source_target_pairs={{24,23}} | collective-permute-start | bytes 3080 | tf_op jit(solution)/shard_map/ppermute | solution.py:316
  40.1 4.8 %collective-permute-start.13 = (f32[1,256]{1,0:T(1,128)S(1)}, f32[1,256]{1,0:T(1,128)S(1)}, u32[]{:S(2)}, u32[]{:S(2)}) collective-permute-start(f32[1,256]{1,0:T(1,128)S(1)} %get-tuple-element.14.nodes), channel_id=1, source_target_pairs={{8,7}} | collective-permute-start | bytes 3080 | tf_op jit(solution)/shard_map/ppermute | solution.py:316

commit v2 on v1

--- a/solution.py
+++ b/solution.py
@@ -173,14 +173,20 @@
             + lower[rest : rest + 1]
         )
 
+    leaving[...] = jnp.zeros_like(leaving)
     for member in range(QUAD):
+
+        @pl.when(lax.rem(place, QUAD) == member)
+        def _():
+            node = width - cut + 1
+            leaving[1:2] = parts[2 * member + 1][node : node + 1]
 
         @pl.when(place == member)
         def _():
             state = parts[2 * member + 1][width - cut : width - cut + 1]
             for k in range(1, QUAD):
                 state = step(state, member ^ k)
-            leaving[...] = state
+            leaving[:1] = state
 
 
 def quad_body(*refs):
@@ -208,15 +214,24 @@
     return lax.rem(lax.div(where_am_i(), QUAD), 2) == 1
 
 
+def is_last():
+    count = lax.axis_size("grp") * lax.axis_size("seg")
+    return where_am_i() >= count - 2 * QUAD
+
+
 def prefix_body(*refs):
-    *parts, far, after, prefix, held = refs
+    *parts, far, late, after, prefix, held = refs
     in_order(held, parts)
     member = lax.rem(where_am_i(), QUAD)
     prefix[...] = held[0]
 
-    @pl.when(jnp.logical_and(is_upper(), where_am_i() >= 2 * QUAD))
+    @pl.when(is_upper() & jnp.logical_not(is_last()) & (where_am_i() >= 2 * QUAD))
     def _():
         put_composed(prefix, far[...], held[0])
+
+    @pl.when(is_upper() & is_last())
+    def _():
+        put_composed(prefix, late[...], held[0])
 
     for k in range(1, QUAD):
 
@@ -225,45 +240,45 @@
             put_composed(prefix, prefix[...], held[k])
 
 
-def follow_body(entry, mapping, out):
-    out[...] = follow(entry[...], mapping[...])
-
-
-def octet_exit_body(entry, own, far, out):
+def quad_exit_body(entry, mapping, out):
+    width = mapping.shape[1]
+    out[...] = jnp.zeros_like(out)
+    out[:1] = follow(entry[:1], mapping[...])
+    out[1:2] = mapping[width + 1 : width + 2]
+
+
+def octet_exit_body(low, high, own, far, out):
     upper = is_upper()
     width = own.shape[1]
-    at = entry[:1]
+    out[...] = jnp.zeros_like(out)
 
     @pl.when(upper)
     def _():
-        out[:1] = follow(follow(at, far[...]), own[...])
+        out[:1] = follow(follow(high[:1], far[...]), own[...])
         out[1:2] = far[width + 1 : width + 2]
 
     @pl.when(jnp.logical_not(upper))
     def _():
-        out[:1] = follow(follow(at, own[...]), far[...])
+        out[:1] = follow(follow(low[:1], own[...]), far[...])
         out[1:2] = own[width + 1 : width + 2]
 
-    out[2:] = jnp.zeros_like(out[2:])
-
-
-def last_body(targets, sources, *refs):
-    *arrived, final, beside, far, back, mapping, out, defect = refs
+
+def last_body(entries, backs, count, *refs):
+    rows = refs[:count]
+    final, beside, far, late, mapping, out, defect = refs[count:]
     place = where_am_i()
     width = out.shape[1]
-    member = lax.rem(place, QUAD)
-    octet = lax.div(place, 2 * QUAD)
+    end = lax.rem(place, QUAD) == QUAD - 1
+    quad = lax.div(place, QUAD)
     entry = jnp.zeros_like(out)
-    following = jnp.where(member == QUAD - 1, far[width + 1 : width + 2], beside[...])
-    following = jnp.where(is_upper() & (member == QUAD - 1), back[...], following)
-    for target, row in zip(targets, arrived):
-        here = octet == target
-        if target == 0:
-            here = jnp.logical_and(here, is_upper())
-        entry = jnp.where(here, row[:1], entry)
-    for source, k in sources:
-        ends = place == 2 * QUAD * (source + 1) - 1
-        following = jnp.where(ends, arrived[k][1:2], following)
+    for target, k in entries:
+        entry = jnp.where(quad == target, rows[k][:1], entry)
+    node = slice(width + 1, width + 2)
+    following = jnp.where(is_last(), late[node], far[node])
+    following = jnp.where(is_upper(), 0.0, following)
+    for target, k in backs:
+        following = jnp.where(quad == target, rows[k][1:2], following)
+    following = jnp.where(end, following, beside[...])
     out[...] = follow(entry, mapping[...])
     defect[...] = final[...] - following
 
@@ -307,41 +322,61 @@
     top3 = swapped(top1, 2)
     bottom3 = swapped(bottom2, 1)
     parts = [top, bottom, top1, bottom1, top2, bottom2, top3, bottom3]
-    (leaving,) = call(first_exit_body, [line], *parts)
-    size = 2 * QUAD
-    octets = segments // size
-
-    def moved(array, start, by, count):
-        pairs = [(start + k, start + k + by) for k in range(count)]
-        return lax.ppermute(array, AXES, pairs)
-
-    row = swapped(leaving, QUAD)
+    wide = ((PAD, width), F32)
     held = pltpu.VMEM((QUAD, *shape[0]), F32)
+    octets = segments // (2 * QUAD)
+
+    def quads_swapped(array, quad_pairs):
+        to = {}
+        for one, two in quad_pairs:
+            for k in range(QUAD):
+                to[one * QUAD + k] = two * QUAD + k
+                to[two * QUAD + k] = one * QUAD + k
+        busy = set(to)
+        for i in range(segments):
+            if i not in busy:
+                core = (i + seg_count) % segments
+                to[i] = i ^ 1 if core in busy else core
+        return lax.ppermute(array, AXES, sorted(to.items()))
+
+    (leaving,) = call(first_exit_body, [wide], *parts)
+    rows, entries, backs = [], [], []
+
+    row = quads_swapped(leaving, [(0, 1)])
+    rows.append(row)
+    entries.append((1, 0))
+    backs.append((0, 0))
     quad, beside = call(quad_body, [shape, line], *parts, leaving, scratch=[held])
-    far = swapped(quad, QUAD)
-    arrived = [(0, row)]
-    (leaving,) = call(follow_body, [line], row, quad)
-    low = moved(leaving, QUAD, QUAD, QUAD)
-    high = moved(leaving, QUAD, size, QUAD)
-    row = high + low
-    arrived.append((1, row))
-    end = (octets - 1) * size
-    last = moved(early[0], end, -1, 1)
-    sources = []
+    far = quads_swapped(quad, [(2 * o, 2 * o + 1) for o in range(1, octets - 1)])
+
+    (leaving,) = call(quad_exit_body, [wide], row, quad)
+    end = 2 * octets - 2
+    high = quads_swapped(leaving, [(1, 3), (end - 1, end)])
+    low = quads_swapped(leaving, [(1, 2)])
+    rows.extend((high, low))
+    entries.extend(((3, 1), (2, 2)))
+    backs.extend(((end - 1, 1), (1, 2)))
+    first = segments - 2 * QUAD
     for octet in range(1, octets - 1):
-        (leaving,) = call(octet_exit_body, [((PAD, width), F32)], row, quad, far)
+        (leaving,) = call(octet_exit_body, [wide], low, high, quad, far)
+        source = 2 * octet
         if octet == octets - 2:
-            row = moved(leaving, octet * size, size, size)
+            pairs = [(i, i + 2 * QUAD) for i in range(first - 2 * QUAD, first)]
+            late = quads_swapped(quad, [(end, end + 1)])
+            low = lax.ppermute(leaving, AXES, pairs)
         else:
-            sources.append((octet, len(arrived)))
-            row = swapped(leaving, (octet ^ (octet + 1)) * size)
-        arrived.append((octet + 1, row))
-    first = moved(early[0], size, -1, 1)
-    (prefix,) = call(prefix_body, [shape], *parts, far, leaving, scratch=[held])
-    targets, rows = zip(*arrived)
+            pairs = [(source, source + 2), (source + 1, source + 3)]
+            low = high = quads_swapped(leaving, pairs)
+            backs.append((source + 1, len(rows)))
+        entries.append((source + 2, len(rows)))
+        entries.append((source + 3, len(rows)))
+        rows.append(low)
+    (prefix,) = call(
+        prefix_body, [shape], *parts, far, late, leaving, scratch=[held]
+    )
     return call(
-        functools.partial(last_body, targets, sources),
-        [line, line], *rows, final, beside, far, first + last, prefix,
+        functools.partial(last_body, entries, backs, len(rows)),
+        [line, line], *rows, final, beside, far, late, prefix,
     )
 
 

time: 47.1 us -> 37.1 us (0.79)
  the two profiles are of different devices: /device:TPU:15 before, /device:TPU:1 now
where the time goes in v2:
time: 37.1 us; the launch traced here: 36.9 us
  starting transfers between devices  18.7 us (50%)
  waiting for transfers between devices  12.6 us (34%)
  Pallas kernels  4.94 us (13%)
  between operations  0.7 us (2%)
    ppermute x6, starting transfers between devices, quads_swapped(): return lax.ppermute(array, AXES, sorted(to.items()))  9.9 us
    ppermute x7, waiting for transfers between devices, swapped(): return lax.ppermute(array, AXES, [(i, i ^ by) for i in range(segments)])  7.81 us
    ppermute x7, starting transfers between devices, swapped(): return lax.ppermute(array, AXES, [(i, i ^ by) for i in range(segments)])  6.93 us
    pallas_call x9, Pallas kernels, call(): pl.pallas_call(body, out_shape=out, in_specs=[HBM if raw else VMEM] * len...  4.94 us
    ppermute x6, waiting for transfers between devices, quads_swapped(): return lax.ppermute(array, AXES, sorted(to.items()))  4.15 us
    ppermute x1, starting transfers between devices, on_device(): low = lax.ppermute(leaving, AXES, pairs)  1.84 us
  transfers between devices with their start and end apart: 14, of which 8 were waited for; matrix products, arithmetic and copies ran while one was open for 0% of the time, Pallas kernels for 6%

profile of v2, /device:TPU:1, one launch (start us, length us, event | category | flops | bytes accessed | tf_op | source)
XLA Modules:
  0.0 36.9 jit_solution(15914418159714715024)
XLA Ops:
  0.7 1.4 %shard_map.68 = (f32[1,256]{1,0:T(1,128)S(1)}, f32[1,256]{1,0:T(1,128)S(1)}, f32[4,256,256]{2,1,0:T(8,128)S(1)}, s32[4,256]{1,0:T(4,128)S(1)}, f32[4,256]{1,0:T(...) custom-call(f32[1,256]{1,0:T(1,128)} %nodes_in.1, f32[1,256]{1,0:T(1,128)} %bitcast.1, f32[4,256,256]{2,1,0:T(8,128)} %jac_in.1, ...), custom_call_target="tpu_custom_call" | custom-call | tf_op jit(solution)/shard_map/pallas_call | solution.py:44
  2.2 1.2 %shard_map.69 = (f32[128,256]{1,0:T(8,128)S(1)}, f32[136,256]{1,0:T(8,128)S(1)}, f32[1,256]{1,0:T(1,128)S(1)}) custom-call(f32[64,256]{1,0:T(8,128)S(1)} %collective-permute-done.other, f32[1,256]{1,0:T(1,128)S(1)} %get-tuple-element.14.nodes, f32[1,256]{1,0:T(1,128)S(1)} %get-tuple-element.15.loss, f32[4,256,256]{2,1,0:T(8,128)S(1)} %get-tuple-element.16.jac, ...), custom_call_target="tpu_custom_call" | custom-call | tf_op jit(solution)/shard_map/pallas_call | solution.py:44
  3.4 2.8 %collective-permute-start.4 = (f32[136,256]{1,0:T(8,128)S(1)}, f32[136,256]{1,0:T(8,128)S(1)}, u32[]{:S(2)}, u32[]{:S(2)}) collective-permute-start(f32[136,256]{1,0:T(8,128)S(1)} %get-tuple-element.22.refs_1_), channel_id=1, source_target_pairs={{0,2},{1,3},{2,0},{3,1},{4,6},{5,7},{6,4},{7,5},{8,10},{9,11},{10,... | collective-permute-start | bytes 417800 | tf_op jit(solution)/shard_map/ppermute | solution.py:294
  6.1 1.2 %collective-permute-start.1 = (f32[128,256]{1,0:T(8,128)S(1)}, f32[128,256]{1,0:T(8,128)S(1)}, u32[]{:S(2)}, u32[]{:S(2)}) collective-permute-start(f32[128,256]{1,0:T(8,128)S(1)} %get-tuple-element.21.refs_0_), channel_id=1, source_target_pairs={{0,1},{1,0},{2,3},{3,2},{4,5},{5,4},{6,7},{7,6},{8,9},{9,8},{10,11... | collective-permute-start | bytes 393224 | tf_op jit(solution)/shard_map/ppermute | solution.py:294
  7.3 0.3 collective-permute-start.2
  7.6 2.5 %collective-permute-done.4.refs_5_ = f32[136,256]{1,0:T(8,128)S(1)} collective-permute-done((f32[136,256]{1,0:T(8,128)S(1)}, f32[136,256]{1,0:T(8,128)S(1)}, u32[]{:S(2)}, u32[]{:S(2)}) %collective-permute-start.4) | collective-permute-done | bytes 139296 | tf_op jit(solution)/shard_map/ppermute | solution.py:294
  10.1 1.2 %collective-permute-start.6 = (f32[136,256]{1,0:T(8,128)S(1)}, f32[136,256]{1,0:T(8,128)S(1)}, u32[]{:S(2)}, u32[]{:S(2)}) collective-permute-start(f32[136,256]{1,0:T(8,128)S(1)} %collective-permute-done.4.refs_5_), channel_id=1, source_target_pairs={{0,1},{1,0},{2,3},{3,2},{4,5},{5,4},{6,7},{7,6},{8,9},{9,8},{10,11... | collective-permute-start | bytes 417800 | tf_op jit(solution)/shard_map/ppermute | solution.py:294
  11.3 1.2 %collective-permute-start.3 = (f32[128,256]{1,0:T(8,128)S(1)}, f32[128,256]{1,0:T(8,128)S(1)}, u32[]{:S(2)}, u32[]{:S(2)}) collective-permute-start(f32[128,256]{1,0:T(8,128)S(1)} %get-tuple-element.21.refs_0_), channel_id=1, source_target_pairs={{0,2},{1,3},{2,0},{3,1},{4,6},{5,7},{6,4},{7,5},{8,10},{9,11},{10,... | collective-permute-start | bytes 393224 | tf_op jit(solution)/shard_map/ppermute | solution.py:294
  12.8 2.6 %collective-permute-done.3.refs_4_ = f32[128,256]{1,0:T(8,128)S(1)} collective-permute-done((f32[128,256]{1,0:T(8,128)S(1)}, f32[128,256]{1,0:T(8,128)S(1)}, u32[]{:S(2)}, u32[]{:S(2)}) %collective-permute-start.3) | collective-permute-done | bytes 131104 | tf_op jit(solution)/shard_map/ppermute | solution.py:294
  15.4 2.6 %collective-permute-done.5.refs_6_ = f32[128,256]{1,0:T(8,128)S(1)} collective-permute-done((f32[128,256]{1,0:T(8,128)S(1)}, f32[128,256]{1,0:T(8,128)S(1)}, u32[]{:S(2)}, u32[]{:S(2)}) %collective-permute-start.5) | collective-permute-done | bytes 131104 | tf_op jit(solution)/shard_map/ppermute | solution.py:294
  18.0 0.9 %shard_map.71 = (f32[264,256]{1,0:T(8,128)S(1)}, f32[1,256]{1,0:T(1,128)S(1)}) custom-call(f32[128,256]{1,0:T(8,128)S(1)} %get-tuple-element.21.refs_0_, f32[136,256]{1,0:T(8,128)S(1)} %get-tuple-element.22.refs_1_, f32[128,256]{1,0:T(8,128)S(1)} %collective-permute-done.1.refs_2_, f32[136,256]{1,0:T(8,128)S(1)} %collective-permute-done.2.refs_3_, ...), custom_call_target="tpu_custom_call" | custom-call | tf_op jit(solution)/shard_map/pallas_call | solution.py:44
  18.9 1.4 %collective-permute-start.10 = (f32[264,256]{1,0:T(8,128)S(1)}, f32[264,256]{1,0:T(8,128)S(1)}, u32[]{:S(2)}, u32[]{:S(2)}) collective-permute-start(f32[264,256]{1,0:T(8,128)S(1)} %get-tuple-element.23.mapping.own), channel_id=1, source_target_pairs={{0,1},{1,0},{2,3},{3,2},{4,5},{5,4},{6,7},{7,6},{8,12},{9,13},{10,... | collective-permute-start | bytes 811016 | tf_op jit(solution)/shard_map/ppermute | solution.py:340
  20.3 0.9 %collective-permute-start.13 = (f32[264,256]{1,0:T(8,128)S(1)}, f32[264,256]{1,0:T(8,128)S(1)}, u32[]{:S(2)}, u32[]{:S(2)}) collective-permute-start(f32[264,256]{1,0:T(8,128)S(1)} %get-tuple-element.23.mapping.own), channel_id=1, source_target_pairs={{0,16},{1,17},{2,18},{3,19},{4,20},{5,21},{6,22},{7,23},{8,9},{9,8... | collective-permute-start | bytes 811016 | tf_op jit(solution)/shard_map/ppermute | solution.py:340
  21.2 1.2 %collective-permute-start.7 = (f32[8,256]{1,0:T(8,128)S(1)}, f32[8,256]{1,0:T(8,128)S(1)}, u32[]{:S(2)}, u32[]{:S(2)}) collective-permute-start(f32[8,256]{1,0:T(8,128)S(1)} %shard_map.70.refs_8_), channel_id=1, source_target_pairs={{0,4},{1,5},{2,6},{3,7},{4,0},{5,1},{6,2},{7,3},{8,24},{9,25},{10,... | collective-permute-start | bytes 24584 | tf_op jit(solution)/shard_map/ppermute | solution.py:340
  22.3 1.7 %collective-permute-done.7.entry.refs_0_ = f32[8,256]{1,0:T(8,128)S(1)} collective-permute-done((f32[8,256]{1,0:T(8,128)S(1)}, f32[8,256]{1,0:T(8,128)S(1)}, u32[]{:S(2)}, u32[]{:S(2)}) %collective-permute-start.7) | collective-permute-done | bytes 8224 | tf_op jit(solution)/shard_map/ppermute | solution.py:340
  24.2 0.9 %collective-permute-start.9 = (f32[8,256]{1,0:T(8,128)S(1)}, f32[8,256]{1,0:T(8,128)S(1)}, u32[]{:S(2)}, u32[]{:S(2)}) collective-permute-start(f32[8,256]{1,0:T(8,128)S(1)} %shard_map.72), channel_id=1, source_target_pairs={{0,16},{1,17},{2,18},{3,19},{4,8},{5,9},{6,10},{7,11},{8,4},{9,5},... | collective-permute-start | bytes 24584 | tf_op jit(solution)/shard_map/ppermute | solution.py:340
  25.2 0.7 %collective-permute-done.9.low.refs_2_ = f32[8,256]{1,0:T(8,128)S(1)} collective-permute-done((f32[8,256]{1,0:T(8,128)S(1)}, f32[8,256]{1,0:T(8,128)S(1)}, u32[]{:S(2)}, u32[]{:S(2)}) %collective-permute-start.9) | collective-permute-done | bytes 8224 | tf_op jit(solution)/shard_map/ppermute | solution.py:340
  25.9 0.3 collective-permute-done.8.high.refs_1_
  26.3 0.2 shard_map.73
  26.5 5.5 %collective-permute-start.11 = (f32[8,256]{1,0:T(8,128)S(1)}, f32[8,256]{1,0:T(8,128)S(1)}, u32[]{:S(2)}, u32[]{:S(2)}) collective-permute-start(f32[8,256]{1,0:T(8,128)S(1)} %shard_map.73), channel_id=1, source_target_pairs={{0,1},{1,0},{2,3},{3,2},{4,5},{5,4},{6,7},{7,6},{8,16},{9,17},{10,... | collective-permute-start | bytes 24584 | tf_op jit(solution)/shard_map/ppermute | solution.py:340
  32.0 1.3 %collective-permute-done.11.low.high.refs_3_ = f32[8,256]{1,0:T(8,128)S(1)} collective-permute-done((f32[8,256]{1,0:T(8,128)S(1)}, f32[8,256]{1,0:T(8,128)S(1)}, u32[]{:S(2)}, u32[]{:S(2)}) %collective-permute-start.11) | collective-permute-done | bytes 8224 | tf_op jit(solution)/shard_map/ppermute | solution.py:340
  33.6 1.8 %collective-permute-start.12 = (f32[8,256]{1,0:T(8,128)S(1)}, f32[8,256]{1,0:T(8,128)S(1)}, u32[]{:S(2)}, u32[]{:S(2)}) collective-permute-start(f32[8,256]{1,0:T(8,128)S(1)} %shard_map.74.refs_10_), channel_id=1, source_target_pairs={{16,24},{17,25},{18,26},{19,27},{20,28},{21,29},{22,30},{23,31}} | collective-permute-start | bytes 24584 | tf_op jit(solution)/shard_map/ppermute | solution.py:366
  35.6 0.6 %collective-permute-done.12.refs_4_ = f32[8,256]{1,0:T(8,128)S(1)} collective-permute-done((f32[8,256]{1,0:T(8,128)S(1)}, f32[8,256]{1,0:T(8,128)S(1)}, u32[]{:S(2)}, u32[]{:S(2)}) %collective-permute-start.12) | collective-permute-done | bytes 8224 | tf_op jit(solution)/shard_map/ppermute | solution.py:366
  36.2 0.7 %shard_map.76 = (f32[1,256]{1,0:T(1,128)}, f32[1,256]{1,0:T(1,128)}) custom-call(f32[8,256]{1,0:T(8,128)S(1)} %collective-permute-done.7.entry.refs_0_, f32[8,256]{1,0:T(8,128)S(1)} %collective-permute-done.8.high.refs_1_, f32[8,256]{1,0:T(8,128)S(1)} %collective-permute-done.9.low.refs_2_, f32[8,256]{1,0:T(8,128)S(1)} %collective-permute-done.11.low.high.refs_3_, ...), custom_call_target="tpu_custom_call" | custom-call | tf_op jit(solution)/shard_map/pallas_call | solution.py:44
  (13 shorter events, 0.9 us)
Async XLA Ops:
  0.6 1.5 %collective-permute-start = (f32[64,256]{1,0:T(8,128)}, f32[64,256]{1,0:T(8,128)S(1)}, u32[]{:S(2)}, u32[]{:S(2)}) collective-permute-start(f32[64,256]{1,0:T(8,128)} %own_in.1), channel_id=1, source_target_pairs={{0,16},{1,17},{2,18},{3,19},{4,20},{5,21},{6,22},{7,23},{8,24},{9,... | collective-permute-start | bytes 196616 | tf_op jit(solution)/shard_map/ppermute | solution.py:294
  3.4 6.8 %collective-permute-start.4 = (f32[136,256]{1,0:T(8,128)S(1)}, f32[136,256]{1,0:T(8,128)S(1)}, u32[]{:S(2)}, u32[]{:S(2)}) collective-permute-start(f32[136,256]{1,0:T(8,128)S(1)} %get-tuple-element.22.refs_1_), channel_id=1, source_target_pairs={{0,2},{1,3},{2,0},{3,1},{4,6},{5,7},{6,4},{7,5},{8,10},{9,11},{10,... | collective-permute-start | bytes 417800 | tf_op jit(solution)/shard_map/ppermute | solution.py:294
  6.1 6.4 %collective-permute-start.1 = (f32[128,256]{1,0:T(8,128)S(1)}, f32[128,256]{1,0:T(8,128)S(1)}, u32[]{:S(2)}, u32[]{:S(2)}) collective-permute-start(f32[128,256]{1,0:T(8,128)S(1)} %get-tuple-element.21.refs_0_), channel_id=1, source_target_pairs={{0,1},{1,0},{2,3},{3,2},{4,5},{5,4},{6,7},{7,6},{8,9},{9,8},{10,11... | collective-permute-start | bytes 393224 | tf_op jit(solution)/shard_map/ppermute | solution.py:294
  7.3 8.1 %collective-permute-start.2 = (f32[136,256]{1,0:T(8,128)S(1)}, f32[136,256]{1,0:T(8,128)S(1)}, u32[]{:S(2)}, u32[]{:S(2)}) collective-permute-start(f32[136,256]{1,0:T(8,128)S(1)} %get-tuple-element.22.refs_1_), channel_id=1, source_target_pairs={{0,1},{1,0},{2,3},{3,2},{4,5},{5,4},{6,7},{7,6},{8,9},{9,8},{10,11... | collective-permute-start | bytes 417800 | tf_op jit(solution)/shard_map/ppermute | solution.py:294
  10.1 7.9 %collective-permute-start.6 = (f32[136,256]{1,0:T(8,128)S(1)}, f32[136,256]{1,0:T(8,128)S(1)}, u32[]{:S(2)}, u32[]{:S(2)}) collective-permute-start(f32[136,256]{1,0:T(8,128)S(1)} %collective-permute-done.4.refs_5_), channel_id=1, source_target_pairs={{0,1},{1,0},{2,3},{3,2},{4,5},{5,4},{6,7},{7,6},{8,9},{9,8},{10,11... | collective-permute-start | bytes 417800 | tf_op jit(solution)/shard_map/ppermute | solution.py:294
  11.3 4.1 %collective-permute-start.3 = (f32[128,256]{1,0:T(8,128)S(1)}, f32[128,256]{1,0:T(8,128)S(1)}, u32[]{:S(2)}, u32[]{:S(2)}) collective-permute-start(f32[128,256]{1,0:T(8,128)S(1)} %get-tuple-element.21.refs_0_), channel_id=1, source_target_pairs={{0,2},{1,3},{2,0},{3,1},{4,6},{5,7},{6,4},{7,5},{8,10},{9,11},{10,... | collective-permute-start | bytes 393224 | tf_op jit(solution)/shard_map/ppermute | solution.py:294
  12.5 5.5 %collective-permute-start.5 = (f32[128,256]{1,0:T(8,128)S(1)}, f32[128,256]{1,0:T(8,128)S(1)}, u32[]{:S(2)}, u32[]{:S(2)}) collective-permute-start(f32[128,256]{1,0:T(8,128)S(1)} %collective-permute-done.1.refs_2_), channel_id=1, source_target_pairs={{0,2},{1,3},{2,0},{3,1},{4,6},{5,7},{6,4},{7,5},{8,10},{9,11},{10,... | collective-permute-start | bytes 393224 | tf_op jit(solution)/shard_map/ppermute | solution.py:294
  18.9 7.4 %collective-permute-start.10 = (f32[264,256]{1,0:T(8,128)S(1)}, f32[264,256]{1,0:T(8,128)S(1)}, u32[]{:S(2)}, u32[]{:S(2)}) collective-permute-start(f32[264,256]{1,0:T(8,128)S(1)} %get-tuple-element.23.mapping.own), channel_id=1, source_target_pairs={{0,1},{1,0},{2,3},{3,2},{4,5},{5,4},{6,7},{7,6},{8,12},{9,13},{10,... | collective-permute-start | bytes 811016 | tf_op jit(solution)/shard_map/ppermute | solution.py:340
  20.3 15.2 %collective-permute-start.13 = (f32[264,256]{1,0:T(8,128)S(1)}, f32[264,256]{1,0:T(8,128)S(1)}, u32[]{:S(2)}, u32[]{:S(2)}) collective-permute-start(f32[264,256]{1,0:T(8,128)S(1)} %get-tuple-element.23.mapping.own), channel_id=1, source_target_pairs={{0,16},{1,17},{2,18},{3,19},{4,20},{5,21},{6,22},{7,23},{8,9},{9,8... | collective-permute-start | bytes 811016 | tf_op jit(solution)/shard_map/ppermute | solution.py:340
  21.2 2.9 %collective-permute-start.7 = (f32[8,256]{1,0:T(8,128)S(1)}, f32[8,256]{1,0:T(8,128)S(1)}, u32[]{:S(2)}, u32[]{:S(2)}) collective-permute-start(f32[8,256]{1,0:T(8,128)S(1)} %shard_map.70.refs_8_), channel_id=1, source_target_pairs={{0,4},{1,5},{2,6},{3,7},{4,0},{5,1},{6,2},{7,3},{8,24},{9,25},{10,... | collective-permute-start | bytes 24584 | tf_op jit(solution)/shard_map/ppermute | solution.py:340
  24.2 1.8 %collective-permute-start.9 = (f32[8,256]{1,0:T(8,128)S(1)}, f32[8,256]{1,0:T(8,128)S(1)}, u32[]{:S(2)}, u32[]{:S(2)}) collective-permute-start(f32[8,256]{1,0:T(8,128)S(1)} %shard_map.72), channel_id=1, source_target_pairs={{0,16},{1,17},{2,18},{3,19},{4,8},{5,9},{6,10},{7,11},{8,4},{9,5},... | collective-permute-start | bytes 24584 | tf_op jit(solution)/shard_map/ppermute | solution.py:340
  25.1 1.2 %collective-permute-start.8 = (f32[8,256]{1,0:T(8,128)S(1)}, f32[8,256]{1,0:T(8,128)S(1)}, u32[]{:S(2)}, u32[]{:S(2)}) collective-permute-start(f32[8,256]{1,0:T(8,128)S(1)} %shard_map.72), channel_id=1, source_target_pairs={{0,16},{1,17},{2,18},{3,19},{4,12},{5,13},{6,14},{7,15},{8,9},{9,8... | collective-permute-start | bytes 24584 | tf_op jit(solution)/shard_map/ppermute | solution.py:340
  26.5 6.8 %collective-permute-start.11 = (f32[8,256]{1,0:T(8,128)S(1)}, f32[8,256]{1,0:T(8,128)S(1)}, u32[]{:S(2)}, u32[]{:S(2)}) collective-permute-start(f32[8,256]{1,0:T(8,128)S(1)} %shard_map.73), channel_id=1, source_target_pairs={{0,1},{1,0},{2,3},{3,2},{4,5},{5,4},{6,7},{7,6},{8,16},{9,17},{10,... | collective-permute-start | bytes 24584 | tf_op jit(solution)/shard_map/ppermute | solution.py:340
  33.6 2.6 %collective-permute-start.12 = (f32[8,256]{1,0:T(8,128)S(1)}, f32[8,256]{1,0:T(8,128)S(1)}, u32[]{:S(2)}, u32[]{:S(2)}) collective-permute-start(f32[8,256]{1,0:T(8,128)S(1)} %shard_map.74.refs_10_), channel_id=1, source_target_pairs={{16,24},{17,25},{18,26},{19,27},{20,28},{21,29},{22,30},{23,31}} | collective-permute-start | bytes 24584 | tf_op jit(solution)/shard_map/ppermute | solution.py:366

commit v3 on v2

--- a/solution.py
+++ b/solution.py
@@ -78,18 +78,16 @@
     nodes, loss, jac, index, near, sens, state, own, sems,
 ):
     steps, width, _ = jac.shape
+    pairs = [(index_in, index), (own_in, own), (nodes_in, nodes), (loss_in, loss)]
+    pairs += [(jac_in.at[k], jac.at[k]) for k in range(steps)]
     copies = [
-        pltpu.make_async_copy(src, dst, sems.at[k])
-        for k, (src, dst) in enumerate(
-            [(nodes_in, nodes), (loss_in, loss), (jac_in.at[0], jac.at[0])]
-            + [(own_in, own), (index_in, index)]
-            + [(jac_in.at[pl.ds(1, steps - 1)], jac.at[pl.ds(1, steps - 1)])]
-        )
+        pltpu.make_async_copy(src, dst, sems.at[k]) for k, (src, dst) in enumerate(pairs)
     ]
     for copy in copies:
         copy.start()
-    for copy in copies[:3]:
+    for copy in copies[:4]:
         copy.wait()
+    near[...] = lookup(own, index, lax.axis_index("grp") * own.shape[0])
     start = jnp.broadcast_to(nodes[...], (PAD, width))
     rates = loss[...]
     slope = jnp.tanh(start)
@@ -97,15 +95,14 @@
     row = lax.broadcasted_iota(jnp.int32, (width, width), 0)
     col = lax.broadcasted_iota(jnp.int32, (width, width), 1)
     first = jnp.where(row == col, weight[:1], 0.0)
+    copies[4].wait()
     both = dot(
         jnp.concatenate([first, -inv_len * rates * slope], axis=0), jac[0], ((1,), (1,))
     )
     sens[...] = jnp.where(row == col, 1.0, 0.0) - both[:width]
     state[...] = start + both[width:]
-    for copy in copies[3:5]:
+    for copy in copies[5:]:
         copy.wait()
-    near[...] = lookup(own, index, lax.axis_index("grp") * own.shape[0])
-    copies[5].wait()
 
 
 def local_body(
@@ -306,7 +303,7 @@
             pltpu.with_memory_space_constraint(array, pltpu.HBM)
             for array in (nodes, loss_rates[None], jac_inverse, rate_table, rate_index)
         ),
-        scratch=[pltpu.VMEM(rate_table.shape, F32), pltpu.SemaphoreType.DMA((6,))],
+        scratch=[pltpu.VMEM(rate_table.shape, F32), pltpu.SemaphoreType.DMA((4 + steps,))],
         raw=True,
     )
     cut = width // 2
@@ -322,7 +319,7 @@
     top3 = swapped(top1, 2)
     bottom3 = swapped(bottom2, 1)
     parts = [top, bottom, top1, bottom1, top2, bottom2, top3, bottom3]
-    wide = ((PAD, width), F32)
+    wide = ((2, width), F32)
     held = pltpu.VMEM((QUAD, *shape[0]), F32)
     octets = segments // (2 * QUAD)
 
@@ -351,11 +348,11 @@
 
     (leaving,) = call(quad_exit_body, [wide], row, quad)
     end = 2 * octets - 2
-    high = quads_swapped(leaving, [(1, 3), (end - 1, end)])
-    low = quads_swapped(leaving, [(1, 2)])
+    high = quads_swapped(leaving, [(1, 3)])
+    low = quads_swapped(leaving, [(1, 2), (end - 1, end)])
     rows.extend((high, low))
     entries.extend(((3, 1), (2, 2)))
-    backs.extend(((end - 1, 1), (1, 2)))
+    backs.extend(((end - 1, 2), (1, 2)))
     first = segments - 2 * QUAD
     for octet in range(1, octets - 1):
         (leaving,) = call(octet_exit_body, [wide], low, high, quad, far)

time: 37.1 us -> 35.8 us (0.965)
  starting transfers between devices: 18.7 us -> 17.6 us
    ppermute x6, starting transfers between devices: 9.9 us -> 8.66 us  [quads_swapped(): return lax.ppermute(array, AXES, sorted(to.items()))]
where the time goes in v3:
time: 35.8 us; the launch traced here: 35.6 us
  starting transfers between devices  17.6 us (49%)
  waiting for transfers between devices  12.3 us (34%)
  Pallas kernels  4.96 us (14%)
  between operations  0.7 us (2%)
    ppermute x6, starting transfers between devices, quads_swapped(): return lax.ppermute(array, AXES, sorted(to.items()))  8.66 us
    ppermute x7, waiting for transfers between devices, swapped(): return lax.ppermute(array, AXES, [(i, i ^ by) for i in range(segments)])  7.83 us
    ppermute x7, starting transfers between devices, swapped(): return lax.ppermute(array, AXES, [(i, i ^ by) for i in range(segments)])  6.95 us
    pallas_call x9, Pallas kernels, call(): pl.pallas_call(body, out_shape=out, in_specs=[HBM if raw else VMEM] * len...  4.96 us
    ppermute x6, waiting for transfers between devices, quads_swapped(): return lax.ppermute(array, AXES, sorted(to.items()))  3.94 us
    ppermute x1, starting transfers between devices, on_device(): low = lax.ppermute(leaving, AXES, pairs)  1.94 us
  transfers between devices with their start and end apart: 14, of which 8 were waited for; matrix products, arithmetic and copies ran while one was open for 0% of the time, Pallas kernels for 6%

profile of v3, /device:TPU:1, one launch (start us, length us, event | category | flops | bytes accessed | tf_op | source)
XLA Modules:
  0.0 35.6 jit_solution(16496739765358628329)
XLA Ops:
  0.7 1.4 %shard_map.68 = (f32[1,256]{1,0:T(1,128)S(1)}, f32[1,256]{1,0:T(1,128)S(1)}, f32[4,256,256]{2,1,0:T(8,128)S(1)}, s32[4,256]{1,0:T(4,128)S(1)}, f32[4,256]{1,0:T(...) custom-call(f32[1,256]{1,0:T(1,128)} %nodes_in.1, f32[1,256]{1,0:T(1,128)} %bitcast.1, f32[4,256,256]{2,1,0:T(8,128)} %jac_in.1, ...), custom_call_target="tpu_custom_call" | custom-call | tf_op jit(solution)/shard_map/pallas_call | solution.py:44
  2.2 1.2 %shard_map.69 = (f32[128,256]{1,0:T(8,128)S(1)}, f32[136,256]{1,0:T(8,128)S(1)}, f32[1,256]{1,0:T(1,128)S(1)}) custom-call(f32[64,256]{1,0:T(8,128)S(1)} %collective-permute-done.other, f32[1,256]{1,0:T(1,128)S(1)} %get-tuple-element.14.nodes, f32[1,256]{1,0:T(1,128)S(1)} %get-tuple-element.15.loss, f32[4,256,256]{2,1,0:T(8,128)S(1)} %get-tuple-element.16.jac, ...), custom_call_target="tpu_custom_call" | custom-call | tf_op jit(solution)/shard_map/pallas_call | solution.py:44
  3.4 2.8 %collective-permute-start.4 = (f32[136,256]{1,0:T(8,128)S(1)}, f32[136,256]{1,0:T(8,128)S(1)}, u32[]{:S(2)}, u32[]{:S(2)}) collective-permute-start(f32[136,256]{1,0:T(8,128)S(1)} %get-tuple-element.22.refs_1_), channel_id=1, source_target_pairs={{0,2},{1,3},{2,0},{3,1},{4,6},{5,7},{6,4},{7,5},{8,10},{9,11},{10,... | collective-permute-start | bytes 417800 | tf_op jit(solution)/shard_map/ppermute | solution.py:291
  6.1 1.2 %collective-permute-start.1 = (f32[128,256]{1,0:T(8,128)S(1)}, f32[128,256]{1,0:T(8,128)S(1)}, u32[]{:S(2)}, u32[]{:S(2)}) collective-permute-start(f32[128,256]{1,0:T(8,128)S(1)} %get-tuple-element.21.refs_0_), channel_id=1, source_target_pairs={{0,1},{1,0},{2,3},{3,2},{4,5},{5,4},{6,7},{7,6},{8,9},{9,8},{10,11... | collective-permute-start | bytes 393224 | tf_op jit(solution)/shard_map/ppermute | solution.py:291
  7.4 0.2 collective-permute-start.2
  7.6 2.6 %collective-permute-done.4.refs_5_ = f32[136,256]{1,0:T(8,128)S(1)} collective-permute-done((f32[136,256]{1,0:T(8,128)S(1)}, f32[136,256]{1,0:T(8,128)S(1)}, u32[]{:S(2)}, u32[]{:S(2)}) %collective-permute-start.4) | collective-permute-done | bytes 139296 | tf_op jit(solution)/shard_map/ppermute | solution.py:291
  10.2 1.2 %collective-permute-start.6 = (f32[136,256]{1,0:T(8,128)S(1)}, f32[136,256]{1,0:T(8,128)S(1)}, u32[]{:S(2)}, u32[]{:S(2)}) collective-permute-start(f32[136,256]{1,0:T(8,128)S(1)} %collective-permute-done.4.refs_5_), channel_id=1, source_target_pairs={{0,1},{1,0},{2,3},{3,2},{4,5},{5,4},{6,7},{7,6},{8,9},{9,8},{10,11... | collective-permute-start | bytes 417800 | tf_op jit(solution)/shard_map/ppermute | solution.py:291
  11.3 1.2 %collective-permute-start.3 = (f32[128,256]{1,0:T(8,128)S(1)}, f32[128,256]{1,0:T(8,128)S(1)}, u32[]{:S(2)}, u32[]{:S(2)}) collective-permute-start(f32[128,256]{1,0:T(8,128)S(1)} %get-tuple-element.21.refs_0_), channel_id=1, source_target_pairs={{0,2},{1,3},{2,0},{3,1},{4,6},{5,7},{6,4},{7,5},{8,10},{9,11},{10,... | collective-permute-start | bytes 393224 | tf_op jit(solution)/shard_map/ppermute | solution.py:291
  12.8 2.6 %collective-permute-done.3.refs_4_ = f32[128,256]{1,0:T(8,128)S(1)} collective-permute-done((f32[128,256]{1,0:T(8,128)S(1)}, f32[128,256]{1,0:T(8,128)S(1)}, u32[]{:S(2)}, u32[]{:S(2)}) %collective-permute-start.3) | collective-permute-done | bytes 131104 | tf_op jit(solution)/shard_map/ppermute | solution.py:291
  15.4 2.6 %collective-permute-done.5.refs_6_ = f32[128,256]{1,0:T(8,128)S(1)} collective-permute-done((f32[128,256]{1,0:T(8,128)S(1)}, f32[128,256]{1,0:T(8,128)S(1)}, u32[]{:S(2)}, u32[]{:S(2)}) %collective-permute-start.5) | collective-permute-done | bytes 131104 | tf_op jit(solution)/shard_map/ppermute | solution.py:291
  18.1 0.9 %shard_map.71 = (f32[264,256]{1,0:T(8,128)S(1)}, f32[1,256]{1,0:T(1,128)S(1)}) custom-call(f32[128,256]{1,0:T(8,128)S(1)} %get-tuple-element.21.refs_0_, f32[136,256]{1,0:T(8,128)S(1)} %get-tuple-element.22.refs_1_, f32[128,256]{1,0:T(8,128)S(1)} %collective-permute-done.1.refs_2_, f32[136,256]{1,0:T(8,128)S(1)} %collective-permute-done.2.refs_3_, ...), custom_call_target="tpu_custom_call" | custom-call | tf_op jit(solution)/shard_map/pallas_call | solution.py:44
  19.0 1.4 %collective-permute-start.10 = (f32[264,256]{1,0:T(8,128)S(1)}, f32[264,256]{1,0:T(8,128)S(1)}, u32[]{:S(2)}, u32[]{:S(2)}) collective-permute-start(f32[264,256]{1,0:T(8,128)S(1)} %get-tuple-element.23.mapping.own), channel_id=1, source_target_pairs={{0,1},{1,0},{2,3},{3,2},{4,5},{5,4},{6,7},{7,6},{8,12},{9,13},{10,... | collective-permute-start | bytes 811016 | tf_op jit(solution)/shard_map/ppermute | solution.py:337
  20.3 0.9 %collective-permute-start.13 = (f32[264,256]{1,0:T(8,128)S(1)}, f32[264,256]{1,0:T(8,128)S(1)}, u32[]{:S(2)}, u32[]{:S(2)}) collective-permute-start(f32[264,256]{1,0:T(8,128)S(1)} %get-tuple-element.23.mapping.own), channel_id=1, source_target_pairs={{0,16},{1,17},{2,18},{3,19},{4,20},{5,21},{6,22},{7,23},{8,9},{9,8... | collective-permute-start | bytes 811016 | tf_op jit(solution)/shard_map/ppermute | solution.py:337
  21.2 1.2 %collective-permute-start.7 = (f32[2,256]{1,0:T(2,128)S(1)}, f32[2,256]{1,0:T(2,128)S(1)}, u32[]{:S(2)}, u32[]{:S(2)}) collective-permute-start(f32[2,256]{1,0:T(2,128)S(1)} %shard_map.70.refs_8_), channel_id=1, source_target_pairs={{0,4},{1,5},{2,6},{3,7},{4,0},{5,1},{6,2},{7,3},{8,24},{9,25},{10,... | collective-permute-start | bytes 6152 | tf_op jit(solution)/shard_map/ppermute | solution.py:337
  22.4 1.6 %collective-permute-done.7.entry.refs_0_ = f32[2,256]{1,0:T(2,128)S(1)} collective-permute-done((f32[2,256]{1,0:T(2,128)S(1)}, f32[2,256]{1,0:T(2,128)S(1)}, u32[]{:S(2)}, u32[]{:S(2)}) %collective-permute-start.7) | collective-permute-done | bytes 2080 | tf_op jit(solution)/shard_map/ppermute | solution.py:337
  24.1 0.9 %collective-permute-start.9 = (f32[2,256]{1,0:T(2,128)S(1)}, f32[2,256]{1,0:T(2,128)S(1)}, u32[]{:S(2)}, u32[]{:S(2)}) collective-permute-start(f32[2,256]{1,0:T(2,128)S(1)} %shard_map.72), channel_id=1, source_target_pairs={{0,16},{1,17},{2,18},{3,19},{4,8},{5,9},{6,10},{7,11},{8,4},{9,5},... | collective-permute-start | bytes 6152 | tf_op jit(solution)/shard_map/ppermute | solution.py:337
  25.1 0.7 %collective-permute-done.9.low.refs_2_ = f32[2,256]{1,0:T(2,128)S(1)} collective-permute-done((f32[2,256]{1,0:T(2,128)S(1)}, f32[2,256]{1,0:T(2,128)S(1)}, u32[]{:S(2)}, u32[]{:S(2)}) %collective-permute-start.9) | collective-permute-done | bytes 2080 | tf_op jit(solution)/shard_map/ppermute | solution.py:337
  25.8 0.3 collective-permute-done.8.high.refs_1_
  26.2 0.2 shard_map.73
  26.4 4.2 %collective-permute-start.11 = (f32[2,256]{1,0:T(2,128)S(1)}, f32[2,256]{1,0:T(2,128)S(1)}, u32[]{:S(2)}, u32[]{:S(2)}) collective-permute-start(f32[2,256]{1,0:T(2,128)S(1)} %shard_map.73), channel_id=1, source_target_pairs={{0,1},{1,0},{2,3},{3,2},{4,5},{5,4},{6,7},{7,6},{8,16},{9,17},{10,... | collective-permute-start | bytes 6152 | tf_op jit(solution)/shard_map/ppermute | solution.py:337
  30.7 1.3 %collective-permute-done.11.low.high.refs_3_ = f32[2,256]{1,0:T(2,128)S(1)} collective-permute-done((f32[2,256]{1,0:T(2,128)S(1)}, f32[2,256]{1,0:T(2,128)S(1)}, u32[]{:S(2)}, u32[]{:S(2)}) %collective-permute-start.11) | collective-permute-done | bytes 2080 | tf_op jit(solution)/shard_map/ppermute | solution.py:337
  32.2 1.9 %collective-permute-start.12 = (f32[2,256]{1,0:T(2,128)S(1)}, f32[2,256]{1,0:T(2,128)S(1)}, u32[]{:S(2)}, u32[]{:S(2)}) collective-permute-start(f32[2,256]{1,0:T(2,128)S(1)} %shard_map.74.refs_10_), channel_id=1, source_target_pairs={{16,24},{17,25},{18,26},{19,27},{20,28},{21,29},{22,30},{23,31}} | collective-permute-start | bytes 6152 | tf_op jit(solution)/shard_map/ppermute | solution.py:363
  34.3 0.6 %collective-permute-done.12.refs_4_ = f32[2,256]{1,0:T(2,128)S(1)} collective-permute-done((f32[2,256]{1,0:T(2,128)S(1)}, f32[2,256]{1,0:T(2,128)S(1)}, u32[]{:S(2)}, u32[]{:S(2)}) %collective-permute-start.12) | collective-permute-done | bytes 2080 | tf_op jit(solution)/shard_map/ppermute | solution.py:363
  34.9 0.7 %shard_map.76 = (f32[1,256]{1,0:T(1,128)}, f32[1,256]{1,0:T(1,128)}) custom-call(f32[2,256]{1,0:T(2,128)S(1)} %collective-permute-done.7.entry.refs_0_, f32[2,256]{1,0:T(2,128)S(1)} %collective-permute-done.8.high.refs_1_, f32[2,256]{1,0:T(2,128)S(1)} %collective-permute-done.9.low.refs_2_, f32[2,256]{1,0:T(2,128)S(1)} %collective-permute-done.11.low.high.refs_3_, ...), custom_call_target="tpu_custom_call" | custom-call | tf_op jit(solution)/shard_map/pallas_call | solution.py:44
  (13 shorter events, 0.9 us)
Async XLA Ops:
  0.6 1.5 %collective-permute-start = (f32[64,256]{1,0:T(8,128)}, f32[64,256]{1,0:T(8,128)S(1)}, u32[]{:S(2)}, u32[]{:S(2)}) collective-permute-start(f32[64,256]{1,0:T(8,128)} %own_in.1), channel_id=1, source_target_pairs={{0,16},{1,17},{2,18},{3,19},{4,20},{5,21},{6,22},{7,23},{8,24},{9,... | collective-permute-start | bytes 196616 | tf_op jit(solution)/shard_map/ppermute | solution.py:291
  3.4 6.8 %collective-permute-start.4 = (f32[136,256]{1,0:T(8,128)S(1)}, f32[136,256]{1,0:T(8,128)S(1)}, u32[]{:S(2)}, u32[]{:S(2)}) collective-permute-start(f32[136,256]{1,0:T(8,128)S(1)} %get-tuple-element.22.refs_1_), channel_id=1, source_target_pairs={{0,2},{1,3},{2,0},{3,1},{4,6},{5,7},{6,4},{7,5},{8,10},{9,11},{10,... | collective-permute-start | bytes 417800 | tf_op jit(solution)/shard_map/ppermute | solution.py:291
  6.1 6.4 %collective-permute-start.1 = (f32[128,256]{1,0:T(8,128)S(1)}, f32[128,256]{1,0:T(8,128)S(1)}, u32[]{:S(2)}, u32[]{:S(2)}) collective-permute-start(f32[128,256]{1,0:T(8,128)S(1)} %get-tuple-element.21.refs_0_), channel_id=1, source_target_pairs={{0,1},{1,0},{2,3},{3,2},{4,5},{5,4},{6,7},{7,6},{8,9},{9,8},{10,11... | collective-permute-start | bytes 393224 | tf_op jit(solution)/shard_map/ppermute | solution.py:291
  7.4 8.1 %collective-permute-start.2 = (f32[136,256]{1,0:T(8,128)S(1)}, f32[136,256]{1,0:T(8,128)S(1)}, u32[]{:S(2)}, u32[]{:S(2)}) collective-permute-start(f32[136,256]{1,0:T(8,128)S(1)} %get-tuple-element.22.refs_1_), channel_id=1, source_target_pairs={{0,1},{1,0},{2,3},{3,2},{4,5},{5,4},{6,7},{7,6},{8,9},{9,8},{10,11... | collective-permute-start | bytes 417800 | tf_op jit(solution)/shard_map/ppermute | solution.py:291
  10.2 7.9 %collective-permute-start.6 = (f32[136,256]{1,0:T(8,128)S(1)}, f32[136,256]{1,0:T(8,128)S(1)}, u32[]{:S(2)}, u32[]{:S(2)}) collective-permute-start(f32[136,256]{1,0:T(8,128)S(1)} %collective-permute-done.4.refs_5_), channel_id=1, source_target_pairs={{0,1},{1,0},{2,3},{3,2},{4,5},{5,4},{6,7},{7,6},{8,9},{9,8},{10,11... | collective-permute-start | bytes 417800 | tf_op jit(solution)/shard_map/ppermute | solution.py:291
  11.3 4.1 %collective-permute-start.3 = (f32[128,256]{1,0:T(8,128)S(1)}, f32[128,256]{1,0:T(8,128)S(1)}, u32[]{:S(2)}, u32[]{:S(2)}) collective-permute-start(f32[128,256]{1,0:T(8,128)S(1)} %get-tuple-element.21.refs_0_), channel_id=1, source_target_pairs={{0,2},{1,3},{2,0},{3,1},{4,6},{5,7},{6,4},{7,5},{8,10},{9,11},{10,... | collective-permute-start | bytes 393224 | tf_op jit(solution)/shard_map/ppermute | solution.py:291
  12.6 5.5 %collective-permute-start.5 = (f32[128,256]{1,0:T(8,128)S(1)}, f32[128,256]{1,0:T(8,128)S(1)}, u32[]{:S(2)}, u32[]{:S(2)}) collective-permute-start(f32[128,256]{1,0:T(8,128)S(1)} %collective-permute-done.1.refs_2_), channel_id=1, source_target_pairs={{0,2},{1,3},{2,0},{3,1},{4,6},{5,7},{6,4},{7,5},{8,10},{9,11},{10,... | collective-permute-start | bytes 393224 | tf_op jit(solution)/shard_map/ppermute | solution.py:291
  19.0 7.2 %collective-permute-start.10 = (f32[264,256]{1,0:T(8,128)S(1)}, f32[264,256]{1,0:T(8,128)S(1)}, u32[]{:S(2)}, u32[]{:S(2)}) collective-permute-start(f32[264,256]{1,0:T(8,128)S(1)} %get-tuple-element.23.mapping.own), channel_id=1, source_target_pairs={{0,1},{1,0},{2,3},{3,2},{4,5},{5,4},{6,7},{7,6},{8,12},{9,13},{10,... | collective-permute-start | bytes 811016 | tf_op jit(solution)/shard_map/ppermute | solution.py:337
  20.3 13.8 %collective-permute-start.13 = (f32[264,256]{1,0:T(8,128)S(1)}, f32[264,256]{1,0:T(8,128)S(1)}, u32[]{:S(2)}, u32[]{:S(2)}) collective-permute-start(f32[264,256]{1,0:T(8,128)S(1)} %get-tuple-element.23.mapping.own), channel_id=1, source_target_pairs={{0,16},{1,17},{2,18},{3,19},{4,20},{5,21},{6,22},{7,23},{8,9},{9,8... | collective-permute-start | bytes 811016 | tf_op jit(solution)/shard_map/ppermute | solution.py:337
  21.2 2.7 %collective-permute-start.7 = (f32[2,256]{1,0:T(2,128)S(1)}, f32[2,256]{1,0:T(2,128)S(1)}, u32[]{:S(2)}, u32[]{:S(2)}) collective-permute-start(f32[2,256]{1,0:T(2,128)S(1)} %shard_map.70.refs_8_), channel_id=1, source_target_pairs={{0,4},{1,5},{2,6},{3,7},{4,0},{5,1},{6,2},{7,3},{8,24},{9,25},{10,... | collective-permute-start | bytes 6152 | tf_op jit(solution)/shard_map/ppermute | solution.py:337
  24.1 1.7 %collective-permute-start.9 = (f32[2,256]{1,0:T(2,128)S(1)}, f32[2,256]{1,0:T(2,128)S(1)}, u32[]{:S(2)}, u32[]{:S(2)}) collective-permute-start(f32[2,256]{1,0:T(2,128)S(1)} %shard_map.72), channel_id=1, source_target_pairs={{0,16},{1,17},{2,18},{3,19},{4,8},{5,9},{6,10},{7,11},{8,4},{9,5},... | collective-permute-start | bytes 6152 | tf_op jit(solution)/shard_map/ppermute | solution.py:337
  25.0 1.2 %collective-permute-start.8 = (f32[2,256]{1,0:T(2,128)S(1)}, f32[2,256]{1,0:T(2,128)S(1)}, u32[]{:S(2)}, u32[]{:S(2)}) collective-permute-start(f32[2,256]{1,0:T(2,128)S(1)} %shard_map.72), channel_id=1, source_target_pairs={{0,16},{1,17},{2,18},{3,19},{4,12},{5,13},{6,14},{7,15},{8,24},{9,... | collective-permute-start | bytes 6152 | tf_op jit(solution)/shard_map/ppermute | solution.py:337
  26.4 5.5 %collective-permute-start.11 = (f32[2,256]{1,0:T(2,128)S(1)}, f32[2,256]{1,0:T(2,128)S(1)}, u32[]{:S(2)}, u32[]{:S(2)}) collective-permute-start(f32[2,256]{1,0:T(2,128)S(1)} %shard_map.73), channel_id=1, source_target_pairs={{0,1},{1,0},{2,3},{3,2},{4,5},{5,4},{6,7},{7,6},{8,16},{9,17},{10,... | collective-permute-start | bytes 6152 | tf_op jit(solution)/shard_map/ppermute | solution.py:337
  32.2 2.7 %collective-permute-start.12 = (f32[2,256]{1,0:T(2,128)S(1)}, f32[2,256]{1,0:T(2,128)S(1)}, u32[]{:S(2)}, u32[]{:S(2)}) collective-permute-start(f32[2,256]{1,0:T(2,128)S(1)} %shard_map.74.refs_10_), channel_id=1, source_target_pairs={{16,24},{17,25},{18,26},{19,27},{20,28},{21,29},{22,30},{23,31}} | collective-permute-start | bytes 6152 | tf_op jit(solution)/shard_map/ppermute | solution.py:363

commit v4 on v3

--- a/solution.py
+++ b/solution.py
@@ -186,13 +186,32 @@
             leaving[:1] = state
 
 
-def quad_body(*refs):
-    *parts, after, total, beside, held = refs
+def join(ref, k, top, bottom):
+    cut = top.shape[0]
+    ref[k, :cut] = top[...]
+    ref[k, cut:] = bottom[...]
+
+
+def pair_body(top, bottom, top1, bottom1, total, held):
     width = total.shape[1]
-    in_order(held, parts)
-    member = lax.rem(where_am_i(), QUAD)
-    node = width + 1
-    beside[...] = held[lax.rem(member + 1, QUAD), node : node + 1]
+    node = slice(width + 1, width + 2)
+    side = lax.rem(where_am_i(), 2)
+    join(held, side, top, bottom)
+    join(held, 1 - side, top1, bottom1)
+    put_composed(total, held[0], held[1])
+    total[node] = held[0, node]
+
+
+def quad_body(pair, bottom1, top2, bottom2, top3, bottom3, total, beside, held):
+    width = total.shape[1]
+    node = slice(width + 1, width + 2)
+    side = lax.rem(where_am_i(), 2)
+    upper = lax.rem(lax.div(where_am_i(), 2), 2) == 1
+    join(held, side, top2, bottom2)
+    join(held, 1 - side, top3, bottom3)
+    end = bottom1.shape[0] - PAD + 1
+    near, far = bottom1[end : end + 1], bottom3[end : end + 1]
+    beside[...] = jnp.where(side == 0, near, far)
 
     @pl.when(where_am_i() < QUAD)
     def _():
@@ -200,11 +219,18 @@
 
     @pl.when(where_am_i() >= QUAD)
     def _():
-        head = held[0, node : node + 1]
-        put_composed(total, held[0], held[1])
-        put_composed(held.at[0], held[2], held[3])
-        put_composed(total, total[...], held[0])
-        total[node : node + 1] = head
+        head = jnp.where(upper, held[0, node], pair[node])
+        put_composed(held.at[2], held[0], held[1])
+
+        @pl.when(upper)
+        def _():
+            put_composed(total, held[2], pair[...])
+
+        @pl.when(jnp.logical_not(upper))
+        def _():
+            put_composed(total, pair[...], held[2])
+
+        total[node] = head
 
 
 def is_upper():
@@ -343,7 +369,10 @@
     rows.append(row)
     entries.append((1, 0))
     backs.append((0, 0))
-    quad, beside = call(quad_body, [shape, line], *parts, leaving, scratch=[held])
+    (pair,) = call(pair_body, [shape], *parts[:4], scratch=[held])
+    quad, beside = call(
+        quad_body, [shape, line], pair, bottom1, top2, bottom2, top3, bottom3, scratch=[held]
+    )
     far = quads_swapped(quad, [(2 * o, 2 * o + 1) for o in range(1, octets - 1)])
 
     (leaving,) = call(quad_exit_body, [wide], row, quad)

time: 35.8 us -> 35.5 us (level)
    pallas_call x9 -> x10, Pallas kernels: 4.96 us -> 5.02 us  [call(): pl.pallas_call(body, out_shape=out, in_specs=[HBM if raw else VMEM] * len...]
  transfers between devices with their start and end apart: 14 -> 14, of which waited for: 8 -> 9; matrix products, arithmetic and copies ran while one was open for 0% -> 0% of each run, Pallas kernels for 6% -> 7%
where the time goes in v4:
time: 35.5 us; the launch traced here: 35.3 us
  starting transfers between devices  17.5 us (49%)
  waiting for transfers between devices  12 us (34%)
  Pallas kernels  5.02 us (14%)
  between operations  0.71 us (2%)
    ppermute x6, starting transfers between devices, quads_swapped(): return lax.ppermute(array, AXES, sorted(to.items()))  8.65 us
    ppermute x7, waiting for transfers between devices, swapped(): return lax.ppermute(array, AXES, [(i, i ^ by) for i in range(segments)])  7.47 us
    ppermute x7, starting transfers between devices, swapped(): return lax.ppermute(array, AXES, [(i, i ^ by) for i in range(segments)])  6.95 us
    pallas_call x10, Pallas kernels, call(): pl.pallas_call(body, out_shape=out, in_specs=[HBM if raw else VMEM] * len...  5.02 us
    ppermute x6, waiting for transfers between devices, quads_swapped(): return lax.ppermute(array, AXES, sorted(to.items()))  3.95 us
    ppermute x1, starting transfers between devices, on_device(): low = lax.ppermute(leaving, AXES, pairs)  1.95 us
  transfers between devices with their start and end apart: 14, of which 9 were waited for; matrix products, arithmetic and copies ran while one was open for 0% of the time, Pallas kernels for 7%

profile of v4, /device:TPU:1, one launch (start us, length us, event | category | flops | bytes accessed | tf_op | source)
XLA Modules:
  0.0 35.3 jit_solution(654377263565383382)
XLA Ops:
  0.7 1.4 %shard_map.68 = (f32[1,256]{1,0:T(1,128)S(1)}, f32[1,256]{1,0:T(1,128)S(1)}, f32[4,256,256]{2,1,0:T(8,128)S(1)}, s32[4,256]{1,0:T(4,128)S(1)}, f32[4,256]{1,0:T(...) custom-call(f32[1,256]{1,0:T(1,128)} %nodes_in.1, f32[1,256]{1,0:T(1,128)} %bitcast.1, f32[4,256,256]{2,1,0:T(8,128)} %jac_in.1, ...), custom_call_target="tpu_custom_call" | custom-call | tf_op jit(solution)/shard_map/pallas_call | solution.py:44
  2.2 1.2 %shard_map.69 = (f32[128,256]{1,0:T(8,128)S(1)}, f32[136,256]{1,0:T(8,128)S(1)}, f32[1,256]{1,0:T(1,128)S(1)}) custom-call(f32[64,256]{1,0:T(8,128)S(1)} %collective-permute-done.other, f32[1,256]{1,0:T(1,128)S(1)} %get-tuple-element.14.nodes, f32[1,256]{1,0:T(1,128)S(1)} %get-tuple-element.15.loss, f32[4,256,256]{2,1,0:T(8,128)S(1)} %get-tuple-element.16.jac, ...), custom_call_target="tpu_custom_call" | custom-call | tf_op jit(solution)/shard_map/pallas_call | solution.py:44
  3.4 2.8 %collective-permute-start.4 = (f32[136,256]{1,0:T(8,128)S(1)}, f32[136,256]{1,0:T(8,128)S(1)}, u32[]{:S(2)}, u32[]{:S(2)}) collective-permute-start(f32[136,256]{1,0:T(8,128)S(1)} %get-tuple-element.22.refs_1_.bottom), channel_id=1, source_target_pairs={{0,2},{1,3},{2,0},{3,1},{4,6},{5,7},{6,4},{7,5},{8,10},{9,11},{10,... | collective-permute-start | bytes 417800 | tf_op jit(solution)/shard_map/ppermute | solution.py:317
  6.1 1.2 %collective-permute-start.1 = (f32[128,256]{1,0:T(8,128)S(1)}, f32[128,256]{1,0:T(8,128)S(1)}, u32[]{:S(2)}, u32[]{:S(2)}) collective-permute-start(f32[128,256]{1,0:T(8,128)S(1)} %get-tuple-element.21.refs_0_.top), channel_id=1, source_target_pairs={{0,1},{1,0},{2,3},{3,2},{4,5},{5,4},{6,7},{7,6},{8,9},{9,8},{10,11... | collective-permute-start | bytes 393224 | tf_op jit(solution)/shard_map/ppermute | solution.py:317
  7.6 2.6 %collective-permute-done.4.refs_5_.bottom2 = f32[136,256]{1,0:T(8,128)S(1)} collective-permute-done((f32[136,256]{1,0:T(8,128)S(1)}, f32[136,256]{1,0:T(8,128)S(1)}, u32[]{:S(2)}, u32[]{:S(2)}) %collective-permute-start.4) | collective-permute-done | bytes 139296 | tf_op jit(solution)/shard_map/ppermute | solution.py:317
  10.2 1.2 %collective-permute-start.6 = (f32[136,256]{1,0:T(8,128)S(1)}, f32[136,256]{1,0:T(8,128)S(1)}, u32[]{:S(2)}, u32[]{:S(2)}) collective-permute-start(f32[136,256]{1,0:T(8,128)S(1)} %collective-permute-done.4.refs_5_.bottom2), channel_id=1, source_target_pairs={{0,1},{1,0},{2,3},{3,2},{4,5},{5,4},{6,7},{7,6},{8,9},{9,8},{10,11... | collective-permute-start | bytes 417800 | tf_op jit(solution)/shard_map/ppermute | solution.py:317
  11.3 1.2 %collective-permute-start.3 = (f32[128,256]{1,0:T(8,128)S(1)}, f32[128,256]{1,0:T(8,128)S(1)}, u32[]{:S(2)}, u32[]{:S(2)}) collective-permute-start(f32[128,256]{1,0:T(8,128)S(1)} %get-tuple-element.21.refs_0_.top), channel_id=1, source_target_pairs={{0,2},{1,3},{2,0},{3,1},{4,6},{5,7},{6,4},{7,5},{8,10},{9,11},{10,... | collective-permute-start | bytes 393224 | tf_op jit(solution)/shard_map/ppermute | solution.py:317
  12.8 1.1 %collective-permute-done.2.refs_3_.bottom1 = f32[136,256]{1,0:T(8,128)S(1)} collective-permute-done((f32[136,256]{1,0:T(8,128)S(1)}, f32[136,256]{1,0:T(8,128)S(1)}, u32[]{:S(2)}, u32[]{:S(2)}) %collective-permute-start.2) | collective-permute-done | bytes 139296 | tf_op jit(solution)/shard_map/ppermute | solution.py:317
  13.9 0.3 shard_map.71.pair
  14.2 1.2 %collective-permute-done.3.refs_4_.top2 = f32[128,256]{1,0:T(8,128)S(1)} collective-permute-done((f32[128,256]{1,0:T(8,128)S(1)}, f32[128,256]{1,0:T(8,128)S(1)}, u32[]{:S(2)}, u32[]{:S(2)}) %collective-permute-start.3) | collective-permute-done | bytes 131104 | tf_op jit(solution)/shard_map/ppermute | solution.py:317
  15.4 2.6 %collective-permute-done.5.refs_6_.top3 = f32[128,256]{1,0:T(8,128)S(1)} collective-permute-done((f32[128,256]{1,0:T(8,128)S(1)}, f32[128,256]{1,0:T(8,128)S(1)}, u32[]{:S(2)}, u32[]{:S(2)}) %collective-permute-start.5) | collective-permute-done | bytes 131104 | tf_op jit(solution)/shard_map/ppermute | solution.py:317
  18.0 0.6 %shard_map.72 = (f32[264,256]{1,0:T(8,128)S(1)}, f32[1,256]{1,0:T(1,128)S(1)}) custom-call(f32[264,256]{1,0:T(8,128)S(1)} %shard_map.71.pair, f32[136,256]{1,0:T(8,128)S(1)} %collective-permute-done.2.refs_3_.bottom1, f32[128,256]{1,0:T(8,128)S(1)} %collective-permute-done.3.refs_4_.top2, f32[136,256]{1,0:T(8,128)S(1)} %collective-permute-done.4.refs_5_.bottom2, ...), custom_call_target="tpu_custom_call" | custom-call | tf_op jit(solution)/shard_map/pallas_call | solution.py:44
  18.7 1.4 %collective-permute-start.10 = (f32[264,256]{1,0:T(8,128)S(1)}, f32[264,256]{1,0:T(8,128)S(1)}, u32[]{:S(2)}, u32[]{:S(2)}) collective-permute-start(f32[264,256]{1,0:T(8,128)S(1)} %get-tuple-element.23.mapping.own), channel_id=1, source_target_pairs={{0,1},{1,0},{2,3},{3,2},{4,5},{5,4},{6,7},{7,6},{8,12},{9,13},{10,... | collective-permute-start | bytes 811016 | tf_op jit(solution)/shard_map/ppermute | solution.py:363
  20.0 0.8 %collective-permute-start.13 = (f32[264,256]{1,0:T(8,128)S(1)}, f32[264,256]{1,0:T(8,128)S(1)}, u32[]{:S(2)}, u32[]{:S(2)}) collective-permute-start(f32[264,256]{1,0:T(8,128)S(1)} %get-tuple-element.23.mapping.own), channel_id=1, source_target_pairs={{0,16},{1,17},{2,18},{3,19},{4,20},{5,21},{6,22},{7,23},{8,9},{9,8... | collective-permute-start | bytes 811016 | tf_op jit(solution)/shard_map/ppermute | solution.py:363
  20.8 1.2 %collective-permute-start.7 = (f32[2,256]{1,0:T(2,128)S(1)}, f32[2,256]{1,0:T(2,128)S(1)}, u32[]{:S(2)}, u32[]{:S(2)}) collective-permute-start(f32[2,256]{1,0:T(2,128)S(1)} %shard_map.70), channel_id=1, source_target_pairs={{0,4},{1,5},{2,6},{3,7},{4,0},{5,1},{6,2},{7,3},{8,24},{9,25},{10,... | collective-permute-start | bytes 6152 | tf_op jit(solution)/shard_map/ppermute | solution.py:363
  22.0 1.6 %collective-permute-done.7.entry.refs_0_ = f32[2,256]{1,0:T(2,128)S(1)} collective-permute-done((f32[2,256]{1,0:T(2,128)S(1)}, f32[2,256]{1,0:T(2,128)S(1)}, u32[]{:S(2)}, u32[]{:S(2)}) %collective-permute-start.7) | collective-permute-done | bytes 2080 | tf_op jit(solution)/shard_map/ppermute | solution.py:363
  23.7 1.4 %collective-permute-start.9 = (f32[2,256]{1,0:T(2,128)S(1)}, f32[2,256]{1,0:T(2,128)S(1)}, u32[]{:S(2)}, u32[]{:S(2)}) collective-permute-start(f32[2,256]{1,0:T(2,128)S(1)} %shard_map.73), channel_id=1, source_target_pairs={{0,16},{1,17},{2,18},{3,19},{4,8},{5,9},{6,10},{7,11},{8,4},{9,5},... | collective-permute-start | bytes 6152 | tf_op jit(solution)/shard_map/ppermute | solution.py:363
  25.1 0.7 %collective-permute-done.9.low.refs_2_ = f32[2,256]{1,0:T(2,128)S(1)} collective-permute-done((f32[2,256]{1,0:T(2,128)S(1)}, f32[2,256]{1,0:T(2,128)S(1)}, u32[]{:S(2)}, u32[]{:S(2)}) %collective-permute-start.9) | collective-permute-done | bytes 2080 | tf_op jit(solution)/shard_map/ppermute | solution.py:363
  25.8 0.3 collective-permute-done.8.high.refs_1_
  26.4 3.9 %collective-permute-start.11 = (f32[2,256]{1,0:T(2,128)S(1)}, f32[2,256]{1,0:T(2,128)S(1)}, u32[]{:S(2)}, u32[]{:S(2)}) collective-permute-start(f32[2,256]{1,0:T(2,128)S(1)} %shard_map.74), channel_id=1, source_target_pairs={{0,1},{1,0},{2,3},{3,2},{4,5},{5,4},{6,7},{7,6},{8,16},{9,17},{10,... | collective-permute-start | bytes 6152 | tf_op jit(solution)/shard_map/ppermute | solution.py:363
  30.4 1.3 %collective-permute-done.11.low.high.refs_3_ = f32[2,256]{1,0:T(2,128)S(1)} collective-permute-done((f32[2,256]{1,0:T(2,128)S(1)}, f32[2,256]{1,0:T(2,128)S(1)}, u32[]{:S(2)}, u32[]{:S(2)}) %collective-permute-start.11) | collective-permute-done | bytes 2080 | tf_op jit(solution)/shard_map/ppermute | solution.py:363
  31.9 1.9 %collective-permute-start.12 = (f32[2,256]{1,0:T(2,128)S(1)}, f32[2,256]{1,0:T(2,128)S(1)}, u32[]{:S(2)}, u32[]{:S(2)}) collective-permute-start(f32[2,256]{1,0:T(2,128)S(1)} %shard_map.75.refs_10_), channel_id=1, source_target_pairs={{16,24},{17,25},{18,26},{19,27},{20,28},{21,29},{22,30},{23,31}} | collective-permute-start | bytes 6152 | tf_op jit(solution)/shard_map/ppermute | solution.py:392
  34.0 0.6 %collective-permute-done.12.refs_4_ = f32[2,256]{1,0:T(2,128)S(1)} collective-permute-done((f32[2,256]{1,0:T(2,128)S(1)}, f32[2,256]{1,0:T(2,128)S(1)}, u32[]{:S(2)}, u32[]{:S(2)}) %collective-permute-start.12) | collective-permute-done | bytes 2080 | tf_op jit(solution)/shard_map/ppermute | solution.py:392
  34.6 0.7 %shard_map.77 = (f32[1,256]{1,0:T(1,128)}, f32[1,256]{1,0:T(1,128)}) custom-call(f32[2,256]{1,0:T(2,128)S(1)} %collective-permute-done.7.entry.refs_0_, f32[2,256]{1,0:T(2,128)S(1)} %collective-permute-done.8.high.refs_1_, f32[2,256]{1,0:T(2,128)S(1)} %collective-permute-done.9.low.refs_2_, f32[2,256]{1,0:T(2,128)S(1)} %collective-permute-done.11.low.high.refs_3_, ...), custom_call_target="tpu_custom_call" | custom-call | tf_op jit(solution)/shard_map/pallas_call | solution.py:44
  (14 shorter events, 1.4 us)
Async XLA Ops:
  0.6 1.5 %collective-permute-start = (f32[64,256]{1,0:T(8,128)}, f32[64,256]{1,0:T(8,128)S(1)}, u32[]{:S(2)}, u32[]{:S(2)}) collective-permute-start(f32[64,256]{1,0:T(8,128)} %own_in.1), channel_id=1, source_target_pairs={{0,16},{1,17},{2,18},{3,19},{4,20},{5,21},{6,22},{7,23},{8,24},{9,... | collective-permute-start | bytes 196616 | tf_op jit(solution)/shard_map/ppermute | solution.py:317
  3.4 6.8 %collective-permute-start.4 = (f32[136,256]{1,0:T(8,128)S(1)}, f32[136,256]{1,0:T(8,128)S(1)}, u32[]{:S(2)}, u32[]{:S(2)}) collective-permute-start(f32[136,256]{1,0:T(8,128)S(1)} %get-tuple-element.22.refs_1_.bottom), channel_id=1, source_target_pairs={{0,2},{1,3},{2,0},{3,1},{4,6},{5,7},{6,4},{7,5},{8,10},{9,11},{10,... | collective-permute-start | bytes 417800 | tf_op jit(solution)/shard_map/ppermute | solution.py:317
  6.1 6.4 %collective-permute-start.1 = (f32[128,256]{1,0:T(8,128)S(1)}, f32[128,256]{1,0:T(8,128)S(1)}, u32[]{:S(2)}, u32[]{:S(2)}) collective-permute-start(f32[128,256]{1,0:T(8,128)S(1)} %get-tuple-element.21.refs_0_.top), channel_id=1, source_target_pairs={{0,1},{1,0},{2,3},{3,2},{4,5},{5,4},{6,7},{7,6},{8,9},{9,8},{10,11... | collective-permute-start | bytes 393224 | tf_op jit(solution)/shard_map/ppermute | solution.py:317
  7.4 6.5 %collective-permute-start.2 = (f32[136,256]{1,0:T(8,128)S(1)}, f32[136,256]{1,0:T(8,128)S(1)}, u32[]{:S(2)}, u32[]{:S(2)}) collective-permute-start(f32[136,256]{1,0:T(8,128)S(1)} %get-tuple-element.22.refs_1_.bottom), channel_id=1, source_target_pairs={{0,1},{1,0},{2,3},{3,2},{4,5},{5,4},{6,7},{7,6},{8,9},{9,8},{10,11... | collective-permute-start | bytes 417800 | tf_op jit(solution)/shard_map/ppermute | solution.py:317
  10.2 7.9 %collective-permute-start.6 = (f32[136,256]{1,0:T(8,128)S(1)}, f32[136,256]{1,0:T(8,128)S(1)}, u32[]{:S(2)}, u32[]{:S(2)}) collective-permute-start(f32[136,256]{1,0:T(8,128)S(1)} %collective-permute-done.4.refs_5_.bottom2), channel_id=1, source_target_pairs={{0,1},{1,0},{2,3},{3,2},{4,5},{5,4},{6,7},{7,6},{8,9},{9,8},{10,11... | collective-permute-start | bytes 417800 | tf_op jit(solution)/shard_map/ppermute | solution.py:317
  11.3 4.1 %collective-permute-start.3 = (f32[128,256]{1,0:T(8,128)S(1)}, f32[128,256]{1,0:T(8,128)S(1)}, u32[]{:S(2)}, u32[]{:S(2)}) collective-permute-start(f32[128,256]{1,0:T(8,128)S(1)} %get-tuple-element.21.refs_0_.top), channel_id=1, source_target_pairs={{0,2},{1,3},{2,0},{3,1},{4,6},{5,7},{6,4},{7,5},{8,10},{9,11},{10,... | collective-permute-start | bytes 393224 | tf_op jit(solution)/shard_map/ppermute | solution.py:317
  12.6 5.5 %collective-permute-start.5 = (f32[128,256]{1,0:T(8,128)S(1)}, f32[128,256]{1,0:T(8,128)S(1)}, u32[]{:S(2)}, u32[]{:S(2)}) collective-permute-start(f32[128,256]{1,0:T(8,128)S(1)} %collective-permute-done.1.refs_2_.top1), channel_id=1, source_target_pairs={{0,2},{1,3},{2,0},{3,1},{4,6},{5,7},{6,4},{7,5},{8,10},{9,11},{10,... | collective-permute-start | bytes 393224 | tf_op jit(solution)/shard_map/ppermute | solution.py:317
  18.7 7.5 %collective-permute-start.10 = (f32[264,256]{1,0:T(8,128)S(1)}, f32[264,256]{1,0:T(8,128)S(1)}, u32[]{:S(2)}, u32[]{:S(2)}) collective-permute-start(f32[264,256]{1,0:T(8,128)S(1)} %get-tuple-element.23.mapping.own), channel_id=1, source_target_pairs={{0,1},{1,0},{2,3},{3,2},{4,5},{5,4},{6,7},{7,6},{8,12},{9,13},{10,... | collective-permute-start | bytes 811016 | tf_op jit(solution)/shard_map/ppermute | solution.py:363
  20.0 13.8 %collective-permute-start.13 = (f32[264,256]{1,0:T(8,128)S(1)}, f32[264,256]{1,0:T(8,128)S(1)}, u32[]{:S(2)}, u32[]{:S(2)}) collective-permute-start(f32[264,256]{1,0:T(8,128)S(1)} %get-tuple-element.23.mapping.own), channel_id=1, source_target_pairs={{0,16},{1,17},{2,18},{3,19},{4,20},{5,21},{6,22},{7,23},{8,9},{9,8... | collective-permute-start | bytes 811016 | tf_op jit(solution)/shard_map/ppermute | solution.py:363
  20.8 2.8 %collective-permute-start.7 = (f32[2,256]{1,0:T(2,128)S(1)}, f32[2,256]{1,0:T(2,128)S(1)}, u32[]{:S(2)}, u32[]{:S(2)}) collective-permute-start(f32[2,256]{1,0:T(2,128)S(1)} %shard_map.70), channel_id=1, source_target_pairs={{0,4},{1,5},{2,6},{3,7},{4,0},{5,1},{6,2},{7,3},{8,24},{9,25},{10,... | collective-permute-start | bytes 6152 | tf_op jit(solution)/shard_map/ppermute | solution.py:363
  23.7 2.2 %collective-permute-start.9 = (f32[2,256]{1,0:T(2,128)S(1)}, f32[2,256]{1,0:T(2,128)S(1)}, u32[]{:S(2)}, u32[]{:S(2)}) collective-permute-start(f32[2,256]{1,0:T(2,128)S(1)} %shard_map.73), channel_id=1, source_target_pairs={{0,16},{1,17},{2,18},{3,19},{4,8},{5,9},{6,10},{7,11},{8,4},{9,5},... | collective-permute-start | bytes 6152 | tf_op jit(solution)/shard_map/ppermute | solution.py:363
  25.0 1.2 %collective-permute-start.8 = (f32[2,256]{1,0:T(2,128)S(1)}, f32[2,256]{1,0:T(2,128)S(1)}, u32[]{:S(2)}, u32[]{:S(2)}) collective-permute-start(f32[2,256]{1,0:T(2,128)S(1)} %shard_map.73), channel_id=1, source_target_pairs={{0,16},{1,17},{2,18},{3,19},{4,12},{5,13},{6,14},{7,15},{8,24},{9,... | collective-permute-start | bytes 6152 | tf_op jit(solution)/shard_map/ppermute | solution.py:363
  26.4 5.2 %collective-permute-start.11 = (f32[2,256]{1,0:T(2,128)S(1)}, f32[2,256]{1,0:T(2,128)S(1)}, u32[]{:S(2)}, u32[]{:S(2)}) collective-permute-start(f32[2,256]{1,0:T(2,128)S(1)} %shard_map.74), channel_id=1, source_target_pairs={{0,1},{1,0},{2,3},{3,2},{4,5},{5,4},{6,7},{7,6},{8,16},{9,17},{10,... | collective-permute-start | bytes 6152 | tf_op jit(solution)/shard_map/ppermute | solution.py:363
  31.9 2.7 %collective-permute-start.12 = (f32[2,256]{1,0:T(2,128)S(1)}, f32[2,256]{1,0:T(2,128)S(1)}, u32[]{:S(2)}, u32[]{:S(2)}) collective-permute-start(f32[2,256]{1,0:T(2,128)S(1)} %shard_map.75.refs_10_), channel_id=1, source_target_pairs={{16,24},{17,25},{18,26},{19,27},{20,28},{21,29},{22,30},{23,31}} | collective-permute-start | bytes 6152 | tf_op jit(solution)/shard_map/ppermute | solution.py:392

commit v5 on v4

--- a/solution.py
+++ b/solution.py
@@ -142,7 +142,8 @@
     member = lax.rem(where_am_i(), QUAD)
     cut = parts[0].shape[0]
     for k in range(QUAD):
-        place = jnp.bitwise_xor(member, k)
+        by = jnp.where(lax.axis_index("grp") == 0, k, 3 - k) if k in (1, 2) else k
+        place = jnp.bitwise_xor(member, by)
         held[place, :cut] = parts[2 * k][...]
         held[place, cut:] = parts[2 * k + 1][...]
 
@@ -192,25 +193,46 @@
     ref[k, cut:] = bottom[...]
 
 
-def pair_body(top, bottom, top1, bottom1, total, held):
+def pair_body(top, bottom, top1, bottom1, top2, bottom2, total, held):
     width = total.shape[1]
     node = slice(width + 1, width + 2)
     side = lax.rem(where_am_i(), 2)
     join(held, side, top, bottom)
-    join(held, 1 - side, top1, bottom1)
+    straight = lax.axis_index("grp") == 0
+
+    @pl.when(straight)
+    def _():
+        join(held, 1 - side, top1, bottom1)
+
+    @pl.when(jnp.logical_not(straight))
+    def _():
+        join(held, 1 - side, top2, bottom2)
+
     put_composed(total, held[0], held[1])
     total[node] = held[0, node]
 
 
-def quad_body(pair, bottom1, top2, bottom2, top3, bottom3, total, beside, held):
+def quad_body(
+    pair, top1, bottom1, top2, bottom2, top3, bottom3, total, beside, held
+):
     width = total.shape[1]
     node = slice(width + 1, width + 2)
     side = lax.rem(where_am_i(), 2)
     upper = lax.rem(lax.div(where_am_i(), 2), 2) == 1
-    join(held, side, top2, bottom2)
+    straight = lax.axis_index("grp") == 0
+
+    @pl.when(straight)
+    def _():
+        join(held, side, top2, bottom2)
+
+    @pl.when(jnp.logical_not(straight))
+    def _():
+        join(held, side, top1, bottom1)
+
     join(held, 1 - side, top3, bottom3)
     end = bottom1.shape[0] - PAD + 1
-    near, far = bottom1[end : end + 1], bottom3[end : end + 1]
+    one, two = bottom1[end : end + 1], bottom2[end : end + 1]
+    near, far = jnp.where(straight, one, two), bottom3[end : end + 1]
     beside[...] = jnp.where(side == 0, near, far)
 
     @pl.when(where_am_i() < QUAD)
@@ -338,12 +360,17 @@
         functools.partial(local_body, inv_len, src_scale),
         [*halves, line], other, *early,
     )
-    top1 = swapped(top, 1)
-    bottom2 = swapped(bottom, 2)
-    bottom1 = swapped(bottom, 1)
-    top2 = swapped(top, 2)
-    top3 = swapped(top1, 2)
-    bottom3 = swapped(bottom2, 1)
+
+    def turned(array, by):
+        pairs = [(i, i ^ (by if i < seg_count else 3 - by)) for i in range(segments)]
+        return lax.ppermute(array, AXES, pairs)
+
+    top1 = turned(top, 1)
+    bottom2 = turned(bottom, 2)
+    bottom1 = turned(bottom, 1)
+    top2 = turned(top, 2)
+    top3 = turned(top1, 2)
+    bottom3 = turned(bottom2, 1)
     parts = [top, bottom, top1, bottom1, top2, bottom2, top3, bottom3]
     wide = ((2, width), F32)
     held = pltpu.VMEM((QUAD, *shape[0]), F32)
@@ -369,9 +396,9 @@
     rows.append(row)
     entries.append((1, 0))
     backs.append((0, 0))
-    (pair,) = call(pair_body, [shape], *parts[:4], scratch=[held])
+    (pair,) = call(pair_body, [shape], *parts[:6], scratch=[held])
     quad, beside = call(
-        quad_body, [shape, line], pair, bottom1, top2, bottom2, top3, bottom3, scratch=[held]
+        quad_body, [shape, line], pair, *parts[2:], scratch=[held]
     )
     far = quads_swapped(quad, [(2 * o, 2 * o + 1) for o in range(1, octets - 1)])
 

time: 35.5 us -> 35.3 us (level)
  starting transfers between devices: 17.5 us -> 19.1 us
  waiting for transfers between devices: 12 us -> 10.4 us
    ppermute x0 -> x6, starting transfers between devices: none -> 8.1 us  [turned(): return lax.ppermute(array, AXES, pairs)]
    ppermute x7 -> x1, waiting for transfers between devices: 7.47 us -> 0.01 us  [swapped(): return lax.ppermute(array, AXES, [(i, i ^ by) for i in range(segments)])]
    ppermute x7 -> x1, starting transfers between devices: 6.95 us -> 0.08 us  [swapped(): return lax.ppermute(array, AXES, [(i, i ^ by) for i in range(segments)])]
    ppermute x0 -> x6, waiting for transfers between devices: none -> 6.47 us  [turned(): return lax.ppermute(array, AXES, pairs)]
    ppermute x6, starting transfers between devices: 8.65 us -> 9.58 us  [quads_swapped(): return lax.ppermute(array, AXES, sorted(to.items()))]
    ppermute x1, starting transfers between devices: 1.95 us -> 1.29 us  [on_device(): low = lax.ppermute(leaving, AXES, pairs)]
    ppermute x6, waiting for transfers between devices: 3.95 us -> 3.33 us  [quads_swapped(): return lax.ppermute(array, AXES, sorted(to.items()))]
  transfers between devices with their start and end apart: 14 -> 14, of which waited for: 9 -> 8; matrix products, arithmetic and copies ran while one was open for 0% -> 0% of each run, Pallas kernels for 7% -> 7%
where the time goes in v5:
time: 35.3 us; the launch traced here: 35.1 us
  starting transfers between devices  19.1 us (54%)
  waiting for transfers between devices  10.4 us (29%)
  Pallas kernels  5 us (14%)
  between operations  0.71 us (2%)
    ppermute x6, starting transfers between devices, quads_swapped(): return lax.ppermute(array, AXES, sorted(to.items()))  9.58 us
    ppermute x6, starting transfers between devices, turned(): return lax.ppermute(array, AXES, pairs)  8.1 us
    ppermute x6, waiting for transfers between devices, turned(): return lax.ppermute(array, AXES, pairs)  6.47 us
    pallas_call x10, Pallas kernels, call(): pl.pallas_call(body, out_shape=out, in_specs=[HBM if raw else VMEM] * len...  5 us
    ppermute x6, waiting for transfers between devices, quads_swapped(): return lax.ppermute(array, AXES, sorted(to.items()))  3.33 us
    ppermute x1, starting transfers between devices, on_device(): low = lax.ppermute(leaving, AXES, pairs)  1.29 us
  transfers between devices with their start and end apart: 14, of which 8 were waited for; matrix products, arithmetic and copies ran while one was open for 0% of the time, Pallas kernels for 7%

profile of v5, /device:TPU:1, one launch (start us, length us, event | category | flops | bytes accessed | tf_op | source)
XLA Modules:
  0.0 35.1 jit_solution(11007210495865451197)
XLA Ops:
  0.7 1.4 %shard_map.68 = (f32[1,256]{1,0:T(1,128)S(1)}, f32[1,256]{1,0:T(1,128)S(1)}, f32[4,256,256]{2,1,0:T(8,128)S(1)}, s32[4,256]{1,0:T(4,128)S(1)}, f32[4,256]{1,0:T(...) custom-call(f32[1,256]{1,0:T(1,128)} %nodes_in.1, f32[1,256]{1,0:T(1,128)} %bitcast.1, f32[4,256,256]{2,1,0:T(8,128)} %jac_in.1, ...), custom_call_target="tpu_custom_call" | custom-call | tf_op jit(solution)/shard_map/pallas_call | solution.py:44
  2.2 1.2 %shard_map.69 = (f32[128,256]{1,0:T(8,128)S(1)}, f32[136,256]{1,0:T(8,128)S(1)}, f32[1,256]{1,0:T(1,128)S(1)}) custom-call(f32[64,256]{1,0:T(8,128)S(1)} %collective-permute-done.other, f32[1,256]{1,0:T(1,128)S(1)} %get-tuple-element.14.nodes, f32[1,256]{1,0:T(1,128)S(1)} %get-tuple-element.15.loss, f32[4,256,256]{2,1,0:T(8,128)S(1)} %get-tuple-element.16.jac, ...), custom_call_target="tpu_custom_call" | custom-call | tf_op jit(solution)/shard_map/pallas_call | solution.py:44
  3.4 2.8 %collective-permute-start.4 = (f32[136,256]{1,0:T(8,128)S(1)}, f32[136,256]{1,0:T(8,128)S(1)}, u32[]{:S(2)}, u32[]{:S(2)}) collective-permute-start(f32[136,256]{1,0:T(8,128)S(1)} %get-tuple-element.22.refs_1_.bottom), channel_id=1, source_target_pairs={{0,2},{1,3},{2,0},{3,1},{4,6},{5,7},{6,4},{7,5},{8,10},{9,11},{10,... | collective-permute-start | bytes 417800 | tf_op jit(solution)/shard_map/ppermute | solution.py:366
  6.1 1.2 %collective-permute-start.1 = (f32[128,256]{1,0:T(8,128)S(1)}, f32[128,256]{1,0:T(8,128)S(1)}, u32[]{:S(2)}, u32[]{:S(2)}) collective-permute-start(f32[128,256]{1,0:T(8,128)S(1)} %get-tuple-element.21.refs_0_.top), channel_id=1, source_target_pairs={{0,1},{1,0},{2,3},{3,2},{4,5},{5,4},{6,7},{7,6},{8,9},{9,8},{10,11... | collective-permute-start | bytes 393224 | tf_op jit(solution)/shard_map/ppermute | solution.py:366
  7.6 1.3 %collective-permute-done.4.refs_5_.bottom2 = f32[136,256]{1,0:T(8,128)S(1)} collective-permute-done((f32[136,256]{1,0:T(8,128)S(1)}, f32[136,256]{1,0:T(8,128)S(1)}, u32[]{:S(2)}, u32[]{:S(2)}) %collective-permute-start.4) | collective-permute-done | bytes 139296 | tf_op jit(solution)/shard_map/ppermute | solution.py:366
  8.9 2.4 %collective-permute-start.6 = (f32[136,256]{1,0:T(8,128)S(1)}, f32[136,256]{1,0:T(8,128)S(1)}, u32[]{:S(2)}, u32[]{:S(2)}) collective-permute-start(f32[136,256]{1,0:T(8,128)S(1)} %collective-permute-done.4.refs_5_.bottom2), channel_id=1, source_target_pairs={{0,1},{1,0},{2,3},{3,2},{4,5},{5,4},{6,7},{7,6},{8,9},{9,8},{10,11... | collective-permute-start | bytes 417800 | tf_op jit(solution)/shard_map/ppermute | solution.py:366
  11.3 0.8 %collective-permute-start.3 = (f32[128,256]{1,0:T(8,128)S(1)}, f32[128,256]{1,0:T(8,128)S(1)}, u32[]{:S(2)}, u32[]{:S(2)}) collective-permute-start(f32[128,256]{1,0:T(8,128)S(1)} %get-tuple-element.21.refs_0_.top), channel_id=1, source_target_pairs={{0,2},{1,3},{2,0},{3,1},{4,6},{5,7},{6,4},{7,5},{8,10},{9,11},{10,... | collective-permute-start | bytes 393224 | tf_op jit(solution)/shard_map/ppermute | solution.py:366
  12.1 0.7 %collective-permute-start.5 = (f32[128,256]{1,0:T(8,128)S(1)}, f32[128,256]{1,0:T(8,128)S(1)}, u32[]{:S(2)}, u32[]{:S(2)}) collective-permute-start(f32[128,256]{1,0:T(8,128)S(1)} %collective-permute-done.1.refs_2_.top1), channel_id=1, source_target_pairs={{0,2},{1,3},{2,0},{3,1},{4,6},{5,7},{6,4},{7,5},{8,10},{9,11},{10,... | collective-permute-start | bytes 393224 | tf_op jit(solution)/shard_map/ppermute | solution.py:366
  12.7 3.9 %collective-permute-done.3.refs_4_.top2 = f32[128,256]{1,0:T(8,128)S(1)} collective-permute-done((f32[128,256]{1,0:T(8,128)S(1)}, f32[128,256]{1,0:T(8,128)S(1)}, u32[]{:S(2)}, u32[]{:S(2)}) %collective-permute-start.3) | collective-permute-done | bytes 131104 | tf_op jit(solution)/shard_map/ppermute | solution.py:366
  16.7 0.3 shard_map.71.pair
  17.0 1.3 %collective-permute-done.5.refs_6_.top3 = f32[128,256]{1,0:T(8,128)S(1)} collective-permute-done((f32[128,256]{1,0:T(8,128)S(1)}, f32[128,256]{1,0:T(8,128)S(1)}, u32[]{:S(2)}, u32[]{:S(2)}) %collective-permute-start.5) | collective-permute-done | bytes 131104 | tf_op jit(solution)/shard_map/ppermute | solution.py:366
  18.3 0.6 %shard_map.72 = (f32[264,256]{1,0:T(8,128)S(1)}, f32[1,256]{1,0:T(1,128)S(1)}) custom-call(f32[264,256]{1,0:T(8,128)S(1)} %shard_map.71.pair, f32[128,256]{1,0:T(8,128)S(1)} %collective-permute-done.1.refs_2_.top1, f32[136,256]{1,0:T(8,128)S(1)} %collective-permute-done.2.refs_3_.bottom1, f32[128,256]{1,0:T(8,128)S(1)} %collective-permute-done.3.refs_4_.top2, ...), custom_call_target="tpu_custom_call" | custom-call | tf_op jit(solution)/shard_map/pallas_call | solution.py:44
  18.9 0.9 %collective-permute-start.10 = (f32[264,256]{1,0:T(8,128)S(1)}, f32[264,256]{1,0:T(8,128)S(1)}, u32[]{:S(2)}, u32[]{:S(2)}) collective-permute-start(f32[264,256]{1,0:T(8,128)S(1)} %get-tuple-element.23.mapping.own), channel_id=1, source_target_pairs={{0,1},{1,0},{2,3},{3,2},{4,5},{5,4},{6,7},{7,6},{8,12},{9,13},{10,... | collective-permute-start | bytes 811016 | tf_op jit(solution)/shard_map/ppermute | solution.py:390
  19.8 1.5 %collective-permute-start.7 = (f32[2,256]{1,0:T(2,128)S(1)}, f32[2,256]{1,0:T(2,128)S(1)}, u32[]{:S(2)}, u32[]{:S(2)}) collective-permute-start(f32[2,256]{1,0:T(2,128)S(1)} %shard_map.70), channel_id=1, source_target_pairs={{0,4},{1,5},{2,6},{3,7},{4,0},{5,1},{6,2},{7,3},{8,24},{9,25},{10,... | collective-permute-start | bytes 6152 | tf_op jit(solution)/shard_map/ppermute | solution.py:390
  21.3 1.0 %collective-permute-done.7.entry.refs_0_ = f32[2,256]{1,0:T(2,128)S(1)} collective-permute-done((f32[2,256]{1,0:T(2,128)S(1)}, f32[2,256]{1,0:T(2,128)S(1)}, u32[]{:S(2)}, u32[]{:S(2)}) %collective-permute-start.7) | collective-permute-done | bytes 2080 | tf_op jit(solution)/shard_map/ppermute | solution.py:390
  22.4 2.2 %collective-permute-start.9 = (f32[2,256]{1,0:T(2,128)S(1)}, f32[2,256]{1,0:T(2,128)S(1)}, u32[]{:S(2)}, u32[]{:S(2)}) collective-permute-start(f32[2,256]{1,0:T(2,128)S(1)} %shard_map.73), channel_id=1, source_target_pairs={{0,16},{1,17},{2,18},{3,19},{4,8},{5,9},{6,10},{7,11},{8,4},{9,5},... | collective-permute-start | bytes 6152 | tf_op jit(solution)/shard_map/ppermute | solution.py:390
  24.7 0.7 %collective-permute-done.9.low.refs_2_ = f32[2,256]{1,0:T(2,128)S(1)} collective-permute-done((f32[2,256]{1,0:T(2,128)S(1)}, f32[2,256]{1,0:T(2,128)S(1)}, u32[]{:S(2)}, u32[]{:S(2)}) %collective-permute-start.9) | collective-permute-done | bytes 2080 | tf_op jit(solution)/shard_map/ppermute | solution.py:390
  25.4 0.3 collective-permute-done.8.high.refs_1_
  25.8 0.2 shard_map.74
  26.0 4.9 %collective-permute-start.11 = (f32[2,256]{1,0:T(2,128)S(1)}, f32[2,256]{1,0:T(2,128)S(1)}, u32[]{:S(2)}, u32[]{:S(2)}) collective-permute-start(f32[2,256]{1,0:T(2,128)S(1)} %shard_map.74), channel_id=1, source_target_pairs={{0,1},{1,0},{2,3},{3,2},{4,5},{5,4},{6,7},{7,6},{8,16},{9,17},{10,... | collective-permute-start | bytes 6152 | tf_op jit(solution)/shard_map/ppermute | solution.py:390
  30.9 1.3 %collective-permute-done.11.low.high.refs_3_ = f32[2,256]{1,0:T(2,128)S(1)} collective-permute-done((f32[2,256]{1,0:T(2,128)S(1)}, f32[2,256]{1,0:T(2,128)S(1)}, u32[]{:S(2)}, u32[]{:S(2)}) %collective-permute-start.11) | collective-permute-done | bytes 2080 | tf_op jit(solution)/shard_map/ppermute | solution.py:390
  32.4 1.3 %collective-permute-start.12 = (f32[2,256]{1,0:T(2,128)S(1)}, f32[2,256]{1,0:T(2,128)S(1)}, u32[]{:S(2)}, u32[]{:S(2)}) collective-permute-start(f32[2,256]{1,0:T(2,128)S(1)} %shard_map.75.refs_10_), channel_id=1, source_target_pairs={{16,24},{17,25},{18,26},{19,27},{20,28},{21,29},{22,30},{23,31}} | collective-permute-start | bytes 6152 | tf_op jit(solution)/shard_map/ppermute | solution.py:419
  33.9 0.6 %collective-permute-done.12.refs_4_ = f32[2,256]{1,0:T(2,128)S(1)} collective-permute-done((f32[2,256]{1,0:T(2,128)S(1)}, f32[2,256]{1,0:T(2,128)S(1)}, u32[]{:S(2)}, u32[]{:S(2)}) %collective-permute-start.12) | collective-permute-done | bytes 2080 | tf_op jit(solution)/shard_map/ppermute | solution.py:419
  34.4 0.7 %shard_map.77 = (f32[1,256]{1,0:T(1,128)}, f32[1,256]{1,0:T(1,128)}) custom-call(f32[2,256]{1,0:T(2,128)S(1)} %collective-permute-done.7.entry.refs_0_, f32[2,256]{1,0:T(2,128)S(1)} %collective-permute-done.8.high.refs_1_, f32[2,256]{1,0:T(2,128)S(1)} %collective-permute-done.9.low.refs_2_, f32[2,256]{1,0:T(2,128)S(1)} %collective-permute-done.11.low.high.refs_3_, ...), custom_call_target="tpu_custom_call" | custom-call | tf_op jit(solution)/shard_map/pallas_call | solution.py:44
  (14 shorter events, 0.9 us)
Async XLA Ops:
  0.6 1.5 %collective-permute-start = (f32[64,256]{1,0:T(8,128)}, f32[64,256]{1,0:T(8,128)S(1)}, u32[]{:S(2)}, u32[]{:S(2)}) collective-permute-start(f32[64,256]{1,0:T(8,128)} %own_in.1), channel_id=1, source_target_pairs={{0,16},{1,17},{2,18},{3,19},{4,20},{5,21},{6,22},{7,23},{8,24},{9,... | collective-permute-start | bytes 196616 | tf_op jit(solution)/shard_map/ppermute | solution.py:339
  3.4 5.5 %collective-permute-start.4 = (f32[136,256]{1,0:T(8,128)S(1)}, f32[136,256]{1,0:T(8,128)S(1)}, u32[]{:S(2)}, u32[]{:S(2)}) collective-permute-start(f32[136,256]{1,0:T(8,128)S(1)} %get-tuple-element.22.refs_1_.bottom), channel_id=1, source_target_pairs={{0,2},{1,3},{2,0},{3,1},{4,6},{5,7},{6,4},{7,5},{8,10},{9,11},{10,... | collective-permute-start | bytes 417800 | tf_op jit(solution)/shard_map/ppermute | solution.py:366
  6.1 5.9 %collective-permute-start.1 = (f32[128,256]{1,0:T(8,128)S(1)}, f32[128,256]{1,0:T(8,128)S(1)}, u32[]{:S(2)}, u32[]{:S(2)}) collective-permute-start(f32[128,256]{1,0:T(8,128)S(1)} %get-tuple-element.21.refs_0_.top), channel_id=1, source_target_pairs={{0,1},{1,0},{2,3},{3,2},{4,5},{5,4},{6,7},{7,6},{8,9},{9,8},{10,11... | collective-permute-start | bytes 393224 | tf_op jit(solution)/shard_map/ppermute | solution.py:366
  7.4 9.3 %collective-permute-start.2 = (f32[136,256]{1,0:T(8,128)S(1)}, f32[136,256]{1,0:T(8,128)S(1)}, u32[]{:S(2)}, u32[]{:S(2)}) collective-permute-start(f32[136,256]{1,0:T(8,128)S(1)} %get-tuple-element.22.refs_1_.bottom), channel_id=1, source_target_pairs={{0,1},{1,0},{2,3},{3,2},{4,5},{5,4},{6,7},{7,6},{8,9},{9,8},{10,11... | collective-permute-start | bytes 417800 | tf_op jit(solution)/shard_map/ppermute | solution.py:366
  8.9 9.4 %collective-permute-start.6 = (f32[136,256]{1,0:T(8,128)S(1)}, f32[136,256]{1,0:T(8,128)S(1)}, u32[]{:S(2)}, u32[]{:S(2)}) collective-permute-start(f32[136,256]{1,0:T(8,128)S(1)} %collective-permute-done.4.refs_5_.bottom2), channel_id=1, source_target_pairs={{0,1},{1,0},{2,3},{3,2},{4,5},{5,4},{6,7},{7,6},{8,9},{9,8},{10,11... | collective-permute-start | bytes 417800 | tf_op jit(solution)/shard_map/ppermute | solution.py:366
  11.3 5.4 %collective-permute-start.3 = (f32[128,256]{1,0:T(8,128)S(1)}, f32[128,256]{1,0:T(8,128)S(1)}, u32[]{:S(2)}, u32[]{:S(2)}) collective-permute-start(f32[128,256]{1,0:T(8,128)S(1)} %get-tuple-element.21.refs_0_.top), channel_id=1, source_target_pairs={{0,2},{1,3},{2,0},{3,1},{4,6},{5,7},{6,4},{7,5},{8,10},{9,11},{10,... | collective-permute-start | bytes 393224 | tf_op jit(solution)/shard_map/ppermute | solution.py:366
  12.1 6.2 %collective-permute-start.5 = (f32[128,256]{1,0:T(8,128)S(1)}, f32[128,256]{1,0:T(8,128)S(1)}, u32[]{:S(2)}, u32[]{:S(2)}) collective-permute-start(f32[128,256]{1,0:T(8,128)S(1)} %collective-permute-done.1.refs_2_.top1), channel_id=1, source_target_pairs={{0,2},{1,3},{2,0},{3,1},{4,6},{5,7},{6,4},{7,5},{8,10},{9,11},{10,... | collective-permute-start | bytes 393224 | tf_op jit(solution)/shard_map/ppermute | solution.py:366
  18.9 6.9 %collective-permute-start.10 = (f32[264,256]{1,0:T(8,128)S(1)}, f32[264,256]{1,0:T(8,128)S(1)}, u32[]{:S(2)}, u32[]{:S(2)}) collective-permute-start(f32[264,256]{1,0:T(8,128)S(1)} %get-tuple-element.23.mapping.own), channel_id=1, source_target_pairs={{0,1},{1,0},{2,3},{3,2},{4,5},{5,4},{6,7},{7,6},{8,12},{9,13},{10,... | collective-permute-start | bytes 811016 | tf_op jit(solution)/shard_map/ppermute | solution.py:390
  19.8 13.9 %collective-permute-start.13 = (f32[264,256]{1,0:T(8,128)S(1)}, f32[264,256]{1,0:T(8,128)S(1)}, u32[]{:S(2)}, u32[]{:S(2)}) collective-permute-start(f32[264,256]{1,0:T(8,128)S(1)} %get-tuple-element.23.mapping.own), channel_id=1, source_target_pairs={{0,16},{1,17},{2,18},{3,19},{4,20},{5,21},{6,22},{7,23},{8,9},{9,8... | collective-permute-start | bytes 811016 | tf_op jit(solution)/shard_map/ppermute | solution.py:390
  19.8 2.5 %collective-permute-start.7 = (f32[2,256]{1,0:T(2,128)S(1)}, f32[2,256]{1,0:T(2,128)S(1)}, u32[]{:S(2)}, u32[]{:S(2)}) collective-permute-start(f32[2,256]{1,0:T(2,128)S(1)} %shard_map.70), channel_id=1, source_target_pairs={{0,4},{1,5},{2,6},{3,7},{4,0},{5,1},{6,2},{7,3},{8,24},{9,25},{10,... | collective-permute-start | bytes 6152 | tf_op jit(solution)/shard_map/ppermute | solution.py:390
  22.4 3.0 %collective-permute-start.9 = (f32[2,256]{1,0:T(2,128)S(1)}, f32[2,256]{1,0:T(2,128)S(1)}, u32[]{:S(2)}, u32[]{:S(2)}) collective-permute-start(f32[2,256]{1,0:T(2,128)S(1)} %shard_map.73), channel_id=1, source_target_pairs={{0,16},{1,17},{2,18},{3,19},{4,8},{5,9},{6,10},{7,11},{8,4},{9,5},... | collective-permute-start | bytes 6152 | tf_op jit(solution)/shard_map/ppermute | solution.py:390
  24.6 1.2 %collective-permute-start.8 = (f32[2,256]{1,0:T(2,128)S(1)}, f32[2,256]{1,0:T(2,128)S(1)}, u32[]{:S(2)}, u32[]{:S(2)}) collective-permute-start(f32[2,256]{1,0:T(2,128)S(1)} %shard_map.73), channel_id=1, source_target_pairs={{0,16},{1,17},{2,18},{3,19},{4,12},{5,13},{6,14},{7,15},{8,24},{9,... | collective-permute-start | bytes 6152 | tf_op jit(solution)/shard_map/ppermute | solution.py:390
  26.0 6.2 %collective-permute-start.11 = (f32[2,256]{1,0:T(2,128)S(1)}, f32[2,256]{1,0:T(2,128)S(1)}, u32[]{:S(2)}, u32[]{:S(2)}) collective-permute-start(f32[2,256]{1,0:T(2,128)S(1)} %shard_map.74), channel_id=1, source_target_pairs={{0,1},{1,0},{2,3},{3,2},{4,5},{5,4},{6,7},{7,6},{8,16},{9,17},{10,... | collective-permute-start | bytes 6152 | tf_op jit(solution)/shard_map/ppermute | solution.py:390
  32.4 2.0 %collective-permute-start.12 = (f32[2,256]{1,0:T(2,128)S(1)}, f32[2,256]{1,0:T(2,128)S(1)}, u32[]{:S(2)}, u32[]{:S(2)}) collective-permute-start(f32[2,256]{1,0:T(2,128)S(1)} %shard_map.75.refs_10_), channel_id=1, source_target_pairs={{16,24},{17,25},{18,26},{19,27},{20,28},{21,29},{22,30},{23,31}} | collective-permute-start | bytes 6152 | tf_op jit(solution)/shard_map/ppermute | solution.py:419

commit v6 on v5

--- a/solution.py
+++ b/solution.py
@@ -288,24 +288,27 @@
 def quad_exit_body(entry, mapping, out):
     width = mapping.shape[1]
     out[...] = jnp.zeros_like(out)
-    out[:1] = follow(entry[:1], mapping[...])
     out[1:2] = mapping[width + 1 : width + 2]
 
-
-def octet_exit_body(low, high, own, far, out):
+    @pl.when(lax.div(where_am_i(), QUAD) == 1)
+    def _():
+        out[:1] = follow(entry[:1], mapping[...])
+
+
+def octet_exit_body(octet, low, high, own, far, out):
     upper = is_upper()
-    width = own.shape[1]
+    inside = lax.div(where_am_i(), 2 * QUAD) == octet
+    node = slice(own.shape[1] + 1, own.shape[1] + 2)
     out[...] = jnp.zeros_like(out)
-
-    @pl.when(upper)
+    out[1:2] = jnp.where(upper, far[node], own[node])
+
+    @pl.when(inside & upper)
     def _():
         out[:1] = follow(follow(high[:1], far[...]), own[...])
-        out[1:2] = far[width + 1 : width + 2]
-
-    @pl.when(jnp.logical_not(upper))
+
+    @pl.when(inside & jnp.logical_not(upper))
     def _():
         out[:1] = follow(follow(low[:1], own[...]), far[...])
-        out[1:2] = own[width + 1 : width + 2]
 
 
 def last_body(entries, backs, count, *refs):
@@ -411,7 +414,8 @@
     backs.extend(((end - 1, 2), (1, 2)))
     first = segments - 2 * QUAD
     for octet in range(1, octets - 1):
-        (leaving,) = call(octet_exit_body, [wide], low, high, quad, far)
+        body = functools.partial(octet_exit_body, octet)
+        (leaving,) = call(body, [wide], low, high, quad, far)
         source = 2 * octet
         if octet == octets - 2:
             pairs = [(i, i + 2 * QUAD) for i in range(first - 2 * QUAD, first)]

time: 35.3 us -> 35.3 us (level)
  transfers between devices with their start and end apart: 14 -> 14, of which waited for: 8 -> 8; matrix products, arithmetic and copies ran while one was open for 0% -> 0% of each run, Pallas kernels for 7% -> 6%
where the time goes in v6:
time: 35.3 us; the launch traced here: 35.1 us
  starting transfers between devices  19.3 us (55%)
  waiting for transfers between devices  10.5 us (30%)
  Pallas kernels  4.65 us (13%)
  between operations  0.71 us (2%)
    ppermute x6, starting transfers between devices, quads_swapped(): return lax.ppermute(array, AXES, sorted(to.items()))  9.85 us
    ppermute x6, starting transfers between devices, turned(): return lax.ppermute(array, AXES, pairs)  8.1 us
    ppermute x6, waiting for transfers between devices, turned(): return lax.ppermute(array, AXES, pairs)  6.47 us
    pallas_call x10, Pallas kernels, call(): pl.pallas_call(body, out_shape=out, in_specs=[HBM if raw else VMEM] * len...  4.65 us
    ppermute x6, waiting for transfers between devices, quads_swapped(): return lax.ppermute(array, AXES, sorted(to.items()))  3.41 us
    ppermute x1, starting transfers between devices, on_device(): low = lax.ppermute(leaving, AXES, pairs)  1.29 us
  transfers between devices with their start and end apart: 14, of which 8 were waited for; matrix products, arithmetic and copies ran while one was open for 0% of the time, Pallas kernels for 6%

profile of v6, /device:TPU:1, one launch (start us, length us, event | category | flops | bytes accessed | tf_op | source)
XLA Modules:
  0.0 35.1 jit_solution(5301152325655786784)
XLA Ops:
  0.7 1.4 %shard_map.68 = (f32[1,256]{1,0:T(1,128)S(1)}, f32[1,256]{1,0:T(1,128)S(1)}, f32[4,256,256]{2,1,0:T(8,128)S(1)}, s32[4,256]{1,0:T(4,128)S(1)}, f32[4,256]{1,0:T(...) custom-call(f32[1,256]{1,0:T(1,128)} %nodes_in.1, f32[1,256]{1,0:T(1,128)} %bitcast.1, f32[4,256,256]{2,1,0:T(8,128)} %jac_in.1, ...), custom_call_target="tpu_custom_call" | custom-call | tf_op jit(solution)/shard_map/pallas_call | solution.py:44
  2.2 1.2 %shard_map.69 = (f32[128,256]{1,0:T(8,128)S(1)}, f32[136,256]{1,0:T(8,128)S(1)}, f32[1,256]{1,0:T(1,128)S(1)}) custom-call(f32[64,256]{1,0:T(8,128)S(1)} %collective-permute-done.other, f32[1,256]{1,0:T(1,128)S(1)} %get-tuple-element.14.nodes, f32[1,256]{1,0:T(1,128)S(1)} %get-tuple-element.15.loss, f32[4,256,256]{2,1,0:T(8,128)S(1)} %get-tuple-element.16.jac, ...), custom_call_target="tpu_custom_call" | custom-call | tf_op jit(solution)/shard_map/pallas_call | solution.py:44
  3.4 2.8 %collective-permute-start.4 = (f32[136,256]{1,0:T(8,128)S(1)}, f32[136,256]{1,0:T(8,128)S(1)}, u32[]{:S(2)}, u32[]{:S(2)}) collective-permute-start(f32[136,256]{1,0:T(8,128)S(1)} %get-tuple-element.22.refs_1_.bottom), channel_id=1, source_target_pairs={{0,2},{1,3},{2,0},{3,1},{4,6},{5,7},{6,4},{7,5},{8,10},{9,11},{10,... | collective-permute-start | bytes 417800 | tf_op jit(solution)/shard_map/ppermute | solution.py:369
  6.1 1.2 %collective-permute-start.1 = (f32[128,256]{1,0:T(8,128)S(1)}, f32[128,256]{1,0:T(8,128)S(1)}, u32[]{:S(2)}, u32[]{:S(2)}) collective-permute-start(f32[128,256]{1,0:T(8,128)S(1)} %get-tuple-element.21.refs_0_.top), channel_id=1, source_target_pairs={{0,1},{1,0},{2,3},{3,2},{4,5},{5,4},{6,7},{7,6},{8,9},{9,8},{10,11... | collective-permute-start | bytes 393224 | tf_op jit(solution)/shard_map/ppermute | solution.py:369
  7.6 1.3 %collective-permute-done.4.refs_5_.bottom2 = f32[136,256]{1,0:T(8,128)S(1)} collective-permute-done((f32[136,256]{1,0:T(8,128)S(1)}, f32[136,256]{1,0:T(8,128)S(1)}, u32[]{:S(2)}, u32[]{:S(2)}) %collective-permute-start.4) | collective-permute-done | bytes 139296 | tf_op jit(solution)/shard_map/ppermute | solution.py:369
  8.9 2.4 %collective-permute-start.6 = (f32[136,256]{1,0:T(8,128)S(1)}, f32[136,256]{1,0:T(8,128)S(1)}, u32[]{:S(2)}, u32[]{:S(2)}) collective-permute-start(f32[136,256]{1,0:T(8,128)S(1)} %collective-permute-done.4.refs_5_.bottom2), channel_id=1, source_target_pairs={{0,1},{1,0},{2,3},{3,2},{4,5},{5,4},{6,7},{7,6},{8,9},{9,8},{10,11... | collective-permute-start | bytes 417800 | tf_op jit(solution)/shard_map/ppermute | solution.py:369
  11.3 0.8 %collective-permute-start.3 = (f32[128,256]{1,0:T(8,128)S(1)}, f32[128,256]{1,0:T(8,128)S(1)}, u32[]{:S(2)}, u32[]{:S(2)}) collective-permute-start(f32[128,256]{1,0:T(8,128)S(1)} %get-tuple-element.21.refs_0_.top), channel_id=1, source_target_pairs={{0,2},{1,3},{2,0},{3,1},{4,6},{5,7},{6,4},{7,5},{8,10},{9,11},{10,... | collective-permute-start | bytes 393224 | tf_op jit(solution)/shard_map/ppermute | solution.py:369
  12.1 0.7 %collective-permute-start.5 = (f32[128,256]{1,0:T(8,128)S(1)}, f32[128,256]{1,0:T(8,128)S(1)}, u32[]{:S(2)}, u32[]{:S(2)}) collective-permute-start(f32[128,256]{1,0:T(8,128)S(1)} %collective-permute-done.1.refs_2_.top1), channel_id=1, source_target_pairs={{0,2},{1,3},{2,0},{3,1},{4,6},{5,7},{6,4},{7,5},{8,10},{9,11},{10,... | collective-permute-start | bytes 393224 | tf_op jit(solution)/shard_map/ppermute | solution.py:369
  12.7 3.9 %collective-permute-done.3.refs_4_.top2 = f32[128,256]{1,0:T(8,128)S(1)} collective-permute-done((f32[128,256]{1,0:T(8,128)S(1)}, f32[128,256]{1,0:T(8,128)S(1)}, u32[]{:S(2)}, u32[]{:S(2)}) %collective-permute-start.3) | collective-permute-done | bytes 131104 | tf_op jit(solution)/shard_map/ppermute | solution.py:369
  16.7 0.3 shard_map.71.pair
  17.0 1.3 %collective-permute-done.5.refs_6_.top3 = f32[128,256]{1,0:T(8,128)S(1)} collective-permute-done((f32[128,256]{1,0:T(8,128)S(1)}, f32[128,256]{1,0:T(8,128)S(1)}, u32[]{:S(2)}, u32[]{:S(2)}) %collective-permute-start.5) | collective-permute-done | bytes 131104 | tf_op jit(solution)/shard_map/ppermute | solution.py:369
  18.3 0.6 %shard_map.72 = (f32[264,256]{1,0:T(8,128)S(1)}, f32[1,256]{1,0:T(1,128)S(1)}) custom-call(f32[264,256]{1,0:T(8,128)S(1)} %shard_map.71.pair, f32[128,256]{1,0:T(8,128)S(1)} %collective-permute-done.1.refs_2_.top1, f32[136,256]{1,0:T(8,128)S(1)} %collective-permute-done.2.refs_3_.bottom1, f32[128,256]{1,0:T(8,128)S(1)} %collective-permute-done.3.refs_4_.top2, ...), custom_call_target="tpu_custom_call" | custom-call | tf_op jit(solution)/shard_map/pallas_call | solution.py:44
  18.9 0.9 %collective-permute-start.10 = (f32[264,256]{1,0:T(8,128)S(1)}, f32[264,256]{1,0:T(8,128)S(1)}, u32[]{:S(2)}, u32[]{:S(2)}) collective-permute-start(f32[264,256]{1,0:T(8,128)S(1)} %get-tuple-element.23.mapping.own), channel_id=1, source_target_pairs={{0,1},{1,0},{2,3},{3,2},{4,5},{5,4},{6,7},{7,6},{8,12},{9,13},{10,... | collective-permute-start | bytes 811016 | tf_op jit(solution)/shard_map/ppermute | solution.py:393
  19.8 1.5 %collective-permute-start.7 = (f32[2,256]{1,0:T(2,128)S(1)}, f32[2,256]{1,0:T(2,128)S(1)}, u32[]{:S(2)}, u32[]{:S(2)}) collective-permute-start(f32[2,256]{1,0:T(2,128)S(1)} %shard_map.70), channel_id=1, source_target_pairs={{0,4},{1,5},{2,6},{3,7},{4,0},{5,1},{6,2},{7,3},{8,24},{9,25},{10,... | collective-permute-start | bytes 6152 | tf_op jit(solution)/shard_map/ppermute | solution.py:393
  21.3 1.0 %collective-permute-done.7.entry.refs_0_ = f32[2,256]{1,0:T(2,128)S(1)} collective-permute-done((f32[2,256]{1,0:T(2,128)S(1)}, f32[2,256]{1,0:T(2,128)S(1)}, u32[]{:S(2)}, u32[]{:S(2)}) %collective-permute-start.7) | collective-permute-done | bytes 2080 | tf_op jit(solution)/shard_map/ppermute | solution.py:393
  22.3 2.1 %collective-permute-start.9 = (f32[2,256]{1,0:T(2,128)S(1)}, f32[2,256]{1,0:T(2,128)S(1)}, u32[]{:S(2)}, u32[]{:S(2)}) collective-permute-start(f32[2,256]{1,0:T(2,128)S(1)} %shard_map.73), channel_id=1, source_target_pairs={{0,16},{1,17},{2,18},{3,19},{4,8},{5,9},{6,10},{7,11},{8,4},{9,5},... | collective-permute-start | bytes 6152 | tf_op jit(solution)/shard_map/ppermute | solution.py:393
  24.4 0.8 %collective-permute-done.9.low.refs_2_ = f32[2,256]{1,0:T(2,128)S(1)} collective-permute-done((f32[2,256]{1,0:T(2,128)S(1)}, f32[2,256]{1,0:T(2,128)S(1)}, u32[]{:S(2)}, u32[]{:S(2)}) %collective-permute-start.9) | collective-permute-done | bytes 2080 | tf_op jit(solution)/shard_map/ppermute | solution.py:393
  25.2 0.3 collective-permute-done.8.high.refs_1_
  25.6 5.3 %collective-permute-start.11 = (f32[2,256]{1,0:T(2,128)S(1)}, f32[2,256]{1,0:T(2,128)S(1)}, u32[]{:S(2)}, u32[]{:S(2)}) collective-permute-start(f32[2,256]{1,0:T(2,128)S(1)} %shard_map.74), channel_id=1, source_target_pairs={{0,1},{1,0},{2,3},{3,2},{4,5},{5,4},{6,7},{7,6},{8,16},{9,17},{10,... | collective-permute-start | bytes 6152 | tf_op jit(solution)/shard_map/ppermute | solution.py:393
  30.9 1.3 %collective-permute-done.11.low.high.refs_3_ = f32[2,256]{1,0:T(2,128)S(1)} collective-permute-done((f32[2,256]{1,0:T(2,128)S(1)}, f32[2,256]{1,0:T(2,128)S(1)}, u32[]{:S(2)}, u32[]{:S(2)}) %collective-permute-start.11) | collective-permute-done | bytes 2080 | tf_op jit(solution)/shard_map/ppermute | solution.py:393
  32.2 0.2 shard_map.75.refs_10_
  32.4 1.3 %collective-permute-start.12 = (f32[2,256]{1,0:T(2,128)S(1)}, f32[2,256]{1,0:T(2,128)S(1)}, u32[]{:S(2)}, u32[]{:S(2)}) collective-permute-start(f32[2,256]{1,0:T(2,128)S(1)} %shard_map.75.refs_10_), channel_id=1, source_target_pairs={{16,24},{17,25},{18,26},{19,27},{20,28},{21,29},{22,30},{23,31}} | collective-permute-start | bytes 6152 | tf_op jit(solution)/shard_map/ppermute | solution.py:423
  33.9 0.6 %collective-permute-done.12.refs_4_ = f32[2,256]{1,0:T(2,128)S(1)} collective-permute-done((f32[2,256]{1,0:T(2,128)S(1)}, f32[2,256]{1,0:T(2,128)S(1)}, u32[]{:S(2)}, u32[]{:S(2)}) %collective-permute-start.12) | collective-permute-done | bytes 2080 | tf_op jit(solution)/shard_map/ppermute | solution.py:423
  34.4 0.7 %shard_map.77 = (f32[1,256]{1,0:T(1,128)}, f32[1,256]{1,0:T(1,128)}) custom-call(f32[2,256]{1,0:T(2,128)S(1)} %collective-permute-done.7.entry.refs_0_, f32[2,256]{1,0:T(2,128)S(1)} %collective-permute-done.8.high.refs_1_, f32[2,256]{1,0:T(2,128)S(1)} %collective-permute-done.9.low.refs_2_, f32[2,256]{1,0:T(2,128)S(1)} %collective-permute-done.11.low.high.refs_3_, ...), custom_call_target="tpu_custom_call" | custom-call | tf_op jit(solution)/shard_map/pallas_call | solution.py:44
  (14 shorter events, 0.5 us)
Async XLA Ops:
  0.6 1.5 %collective-permute-start = (f32[64,256]{1,0:T(8,128)}, f32[64,256]{1,0:T(8,128)S(1)}, u32[]{:S(2)}, u32[]{:S(2)}) collective-permute-start(f32[64,256]{1,0:T(8,128)} %own_in.1), channel_id=1, source_target_pairs={{0,16},{1,17},{2,18},{3,19},{4,20},{5,21},{6,22},{7,23},{8,24},{9,... | collective-permute-start | bytes 196616 | tf_op jit(solution)/shard_map/ppermute | solution.py:342
  3.4 5.5 %collective-permute-start.4 = (f32[136,256]{1,0:T(8,128)S(1)}, f32[136,256]{1,0:T(8,128)S(1)}, u32[]{:S(2)}, u32[]{:S(2)}) collective-permute-start(f32[136,256]{1,0:T(8,128)S(1)} %get-tuple-element.22.refs_1_.bottom), channel_id=1, source_target_pairs={{0,2},{1,3},{2,0},{3,1},{4,6},{5,7},{6,4},{7,5},{8,10},{9,11},{10,... | collective-permute-start | bytes 417800 | tf_op jit(solution)/shard_map/ppermute | solution.py:369
  6.1 5.9 %collective-permute-start.1 = (f32[128,256]{1,0:T(8,128)S(1)}, f32[128,256]{1,0:T(8,128)S(1)}, u32[]{:S(2)}, u32[]{:S(2)}) collective-permute-start(f32[128,256]{1,0:T(8,128)S(1)} %get-tuple-element.21.refs_0_.top), channel_id=1, source_target_pairs={{0,1},{1,0},{2,3},{3,2},{4,5},{5,4},{6,7},{7,6},{8,9},{9,8},{10,11... | collective-permute-start | bytes 393224 | tf_op jit(solution)/shard_map/ppermute | solution.py:369
  7.4 9.3 %collective-permute-start.2 = (f32[136,256]{1,0:T(8,128)S(1)}, f32[136,256]{1,0:T(8,128)S(1)}, u32[]{:S(2)}, u32[]{:S(2)}) collective-permute-start(f32[136,256]{1,0:T(8,128)S(1)} %get-tuple-element.22.refs_1_.bottom), channel_id=1, source_target_pairs={{0,1},{1,0},{2,3},{3,2},{4,5},{5,4},{6,7},{7,6},{8,9},{9,8},{10,11... | collective-permute-start | bytes 417800 | tf_op jit(solution)/shard_map/ppermute | solution.py:369
  8.9 9.4 %collective-permute-start.6 = (f32[136,256]{1,0:T(8,128)S(1)}, f32[136,256]{1,0:T(8,128)S(1)}, u32[]{:S(2)}, u32[]{:S(2)}) collective-permute-start(f32[136,256]{1,0:T(8,128)S(1)} %collective-permute-done.4.refs_5_.bottom2), channel_id=1, source_target_pairs={{0,1},{1,0},{2,3},{3,2},{4,5},{5,4},{6,7},{7,6},{8,9},{9,8},{10,11... | collective-permute-start | bytes 417800 | tf_op jit(solution)/shard_map/ppermute | solution.py:369
  11.3 5.4 %collective-permute-start.3 = (f32[128,256]{1,0:T(8,128)S(1)}, f32[128,256]{1,0:T(8,128)S(1)}, u32[]{:S(2)}, u32[]{:S(2)}) collective-permute-start(f32[128,256]{1,0:T(8,128)S(1)} %get-tuple-element.21.refs_0_.top), channel_id=1, source_target_pairs={{0,2},{1,3},{2,0},{3,1},{4,6},{5,7},{6,4},{7,5},{8,10},{9,11},{10,... | collective-permute-start | bytes 393224 | tf_op jit(solution)/shard_map/ppermute | solution.py:369
  12.1 6.2 %collective-permute-start.5 = (f32[128,256]{1,0:T(8,128)S(1)}, f32[128,256]{1,0:T(8,128)S(1)}, u32[]{:S(2)}, u32[]{:S(2)}) collective-permute-start(f32[128,256]{1,0:T(8,128)S(1)} %collective-permute-done.1.refs_2_.top1), channel_id=1, source_target_pairs={{0,2},{1,3},{2,0},{3,1},{4,6},{5,7},{6,4},{7,5},{8,10},{9,11},{10,... | collective-permute-start | bytes 393224 | tf_op jit(solution)/shard_map/ppermute | solution.py:369
  18.9 6.7 %collective-permute-start.10 = (f32[264,256]{1,0:T(8,128)S(1)}, f32[264,256]{1,0:T(8,128)S(1)}, u32[]{:S(2)}, u32[]{:S(2)}) collective-permute-start(f32[264,256]{1,0:T(8,128)S(1)} %get-tuple-element.23.mapping.own), channel_id=1, source_target_pairs={{0,1},{1,0},{2,3},{3,2},{4,5},{5,4},{6,7},{7,6},{8,12},{9,13},{10,... | collective-permute-start | bytes 811016 | tf_op jit(solution)/shard_map/ppermute | solution.py:393
  19.8 13.9 %collective-permute-start.13 = (f32[264,256]{1,0:T(8,128)S(1)}, f32[264,256]{1,0:T(8,128)S(1)}, u32[]{:S(2)}, u32[]{:S(2)}) collective-permute-start(f32[264,256]{1,0:T(8,128)S(1)} %get-tuple-element.23.mapping.own), channel_id=1, source_target_pairs={{0,16},{1,17},{2,18},{3,19},{4,20},{5,21},{6,22},{7,23},{8,9},{9,8... | collective-permute-start | bytes 811016 | tf_op jit(solution)/shard_map/ppermute | solution.py:393
  19.8 2.5 %collective-permute-start.7 = (f32[2,256]{1,0:T(2,128)S(1)}, f32[2,256]{1,0:T(2,128)S(1)}, u32[]{:S(2)}, u32[]{:S(2)}) collective-permute-start(f32[2,256]{1,0:T(2,128)S(1)} %shard_map.70), channel_id=1, source_target_pairs={{0,4},{1,5},{2,6},{3,7},{4,0},{5,1},{6,2},{7,3},{8,24},{9,25},{10,... | collective-permute-start | bytes 6152 | tf_op jit(solution)/shard_map/ppermute | solution.py:393
  22.3 2.9 %collective-permute-start.9 = (f32[2,256]{1,0:T(2,128)S(1)}, f32[2,256]{1,0:T(2,128)S(1)}, u32[]{:S(2)}, u32[]{:S(2)}) collective-permute-start(f32[2,256]{1,0:T(2,128)S(1)} %shard_map.73), channel_id=1, source_target_pairs={{0,16},{1,17},{2,18},{3,19},{4,8},{5,9},{6,10},{7,11},{8,4},{9,5},... | collective-permute-start | bytes 6152 | tf_op jit(solution)/shard_map/ppermute | solution.py:393
  24.4 1.2 %collective-permute-start.8 = (f32[2,256]{1,0:T(2,128)S(1)}, f32[2,256]{1,0:T(2,128)S(1)}, u32[]{:S(2)}, u32[]{:S(2)}) collective-permute-start(f32[2,256]{1,0:T(2,128)S(1)} %shard_map.73), channel_id=1, source_target_pairs={{0,16},{1,17},{2,18},{3,19},{4,12},{5,13},{6,14},{7,15},{8,24},{9,... | collective-permute-start | bytes 6152 | tf_op jit(solution)/shard_map/ppermute | solution.py:393
  25.6 6.6 %collective-permute-start.11 = (f32[2,256]{1,0:T(2,128)S(1)}, f32[2,256]{1,0:T(2,128)S(1)}, u32[]{:S(2)}, u32[]{:S(2)}) collective-permute-start(f32[2,256]{1,0:T(2,128)S(1)} %shard_map.74), channel_id=1, source_target_pairs={{0,1},{1,0},{2,3},{3,2},{4,5},{5,4},{6,7},{7,6},{8,16},{9,17},{10,... | collective-permute-start | bytes 6152 | tf_op jit(solution)/shard_map/ppermute | solution.py:393
  32.4 2.0 %collective-permute-start.12 = (f32[2,256]{1,0:T(2,128)S(1)}, f32[2,256]{1,0:T(2,128)S(1)}, u32[]{:S(2)}, u32[]{:S(2)}) collective-permute-start(f32[2,256]{1,0:T(2,128)S(1)} %shard_map.75.refs_10_), channel_id=1, source_target_pairs={{16,24},{17,25},{18,26},{19,27},{20,28},{21,29},{22,30},{23,31}} | collective-permute-start | bytes 6152 | tf_op jit(solution)/shard_map/ppermute | solution.py:423
